TPU v7x, 32 devices: a whole 2x2x4 slice. The times are simulated.
32 devices in a mesh: seq: 8 (over z, y), chan: 4 (over x, core).
Axes of the slice: x: 2, y: 2, z: 4, core: 2. Of those that a mesh axis runs over, the one named last changes fastest.
Arguments:
- proj_in: bfloat16 [3, 1024, 4096], P(None, 'seq', 'chan'), may hold values from -6 to 6
- taps: float32 [3, 3, 4096], P(None, None, 'chan'), may hold values from -3 to 3
- long_filter: float32 [1024, 256], P('seq'), may hold values from -6 to 6
- out_grad: bfloat16 [1024, 4096], P('seq', 'chan'), may hold values from -0.1875 to 0.1875
Outputs:
- input_grad: bfloat16 [3, 1024, 4096], P(None, 'seq', 'chan')
- long_grad: float32 [1024, 256], P('seq', 'chan')
- tap_grad: float32 [3, 3, 4096], P(None, None, 'chan')
All inputs are finite; a program needn't handle non-finite values.
Results may differ from a plain program's by a relative error of at most 0.001.
Values may be sent and summed in bfloat16 or wider, within the bound.
A program may use at most 64 MiB of HBM per device.

v0:
```python
import math

import jax
import jax.numpy as jnp
from jax import lax
from jax.sharding import PartitionSpec as P


def shifted(x, axis, by):
    devices = lax.axis_size(axis)
    pairs = [(i, i + by) for i in range(devices) if 0 <= i + by < devices]
    return lax.ppermute(x, axis, pairs)


def angle_table(left_index, right_index, period):
    product = left_index[:, None] * right_index[None, :] % period
    phase = product.astype(jnp.float32) * (2.0 * math.pi / period)
    return (jnp.cos(phase), jnp.sin(phase))


def contract(pattern, factor_table, operand):
    return jnp.einsum(pattern, factor_table, operand, precision=lax.Precision.HIGHEST)


def steps_of(count):
    return jnp.arange(count, dtype=jnp.int32)


def whole_forward(signal, seq_width):
    tok_rows, stack_count, channels = signal.shape
    period = 2 * seq_width * tok_rows
    narrow = channels // seq_width
    arrived = lax.all_to_all(signal, "seq", split_axis=2, concat_axis=0, tiled=True)
    laid = arrived.reshape(seq_width, tok_rows, stack_count, narrow).transpose(2, 3, 0, 1)
    cos_step, sin_step = angle_table(steps_of(2 * seq_width), steps_of(seq_width), 2 * seq_width)
    real_part = contract("qm,ncmj->ncqj", cos_step, laid)
    imag_part = -contract("qm,ncmj->ncqj", sin_step, laid)
    cos_turn, sin_turn = angle_table(steps_of(2 * seq_width), steps_of(tok_rows), period)
    turned_re = real_part * cos_turn + imag_part * sin_turn
    turned_im = imag_part * cos_turn - real_part * sin_turn
    cos_row, sin_row = angle_table(steps_of(tok_rows), steps_of(tok_rows), tok_rows)
    spec_re = contract("rj,ncqj->ncqr", cos_row, turned_re) + contract(
        "rj,ncqj->ncqr", sin_row, turned_im
    )
    spec_im = contract("rj,ncqj->ncqr", cos_row, turned_im) - contract(
        "rj,ncqj->ncqr", sin_row, turned_re
    )
    return (spec_re, spec_im)


def whole_inverse(spec_re, spec_im, seq_width):
    stack_count, narrow, freq_count, tok_rows = spec_re.shape
    period = 2 * seq_width * tok_rows
    cos_row, sin_row = angle_table(steps_of(tok_rows), steps_of(tok_rows), tok_rows)
    back_re = contract("rj,ncqr->ncqj", cos_row, spec_re) - contract(
        "rj,ncqr->ncqj", sin_row, spec_im
    )
    back_im = contract("rj,ncqr->ncqj", sin_row, spec_re) + contract(
        "rj,ncqr->ncqj", cos_row, spec_im
    )
    cos_turn, sin_turn = angle_table(steps_of(freq_count), steps_of(tok_rows), period)
    turned_re = back_re * cos_turn - back_im * sin_turn
    turned_im = back_re * sin_turn + back_im * cos_turn
    cos_step, sin_step = angle_table(steps_of(seq_width), steps_of(freq_count), freq_count)
    signal = contract("mq,ncqj->ncmj", cos_step, turned_re) - contract(
        "mq,ncqj->ncmj", sin_step, turned_im
    )
    signal = (
        (signal / period).transpose(2, 3, 0, 1).reshape(seq_width * tok_rows, stack_count, narrow)
    )
    return lax.all_to_all(signal, "seq", split_axis=0, concat_axis=2, tiled=True)


def member(values, index, stack_axis):
    return lax.index_in_dim(values, index, stack_axis, keepdims=False)


def shards(proj_in, taps, long_filter, out_grad):
    stream_count, tok_rows, channels = proj_in.shape
    tap_count = taps.shape[1]
    groups = long_filter.shape[1]
    seq_width = lax.axis_size("seq")
    lower_rim = shifted(proj_in[:, tok_rows - (tap_count - 1) :, :], "seq", 1)
    extended = jnp.concatenate([lower_rim, proj_in], axis=1).astype(jnp.float32)
    lagged = [
        extended[:, tap_count - 1 - lag_step : tap_count - 1 - lag_step + tok_rows, :]
        for lag_step in range(tap_count)
    ]
    featured = taps[:, 0, None, :] * lagged[0]
    for lag_step in range(1, tap_count):
        featured = featured + taps[:, lag_step, None, :] * lagged[lag_step]
    query_rows, key_rows, value_rows = (featured[0], featured[1], featured[2])
    mixed_rows = key_rows * value_rows
    upstream = out_grad.astype(jnp.float32)
    conv_grad = upstream * query_rows
    tiled_filter = jnp.tile(long_filter, (1, channels // groups))
    signals = jnp.stack([mixed_rows, conv_grad, tiled_filter], axis=1)
    data_re, data_im = whole_forward(signals, seq_width)
    stack_axis = 0
    mix_re, mix_im = (member(data_re, 0, stack_axis), member(data_im, 0, stack_axis))
    grad_re, grad_im = (member(data_re, 1, stack_axis), member(data_im, 1, stack_axis))
    filt_re, filt_im = (member(data_re, 2, stack_axis), member(data_im, 2, stack_axis))
    conv_re = filt_re * mix_re - filt_im * mix_im
    conv_im = filt_re * mix_im + filt_im * mix_re
    back_re = filt_re * grad_re + filt_im * grad_im
    back_im = filt_re * grad_im - filt_im * grad_re
    corr_re = grad_re * mix_re + grad_im * mix_im
    corr_im = grad_im * mix_re - grad_re * mix_im
    prod_re = jnp.stack([conv_re, back_re, corr_re], axis=stack_axis)
    prod_im = jnp.stack([conv_im, back_im, corr_im], axis=stack_axis)
    outputs = whole_inverse(prod_re, prod_im, seq_width)
    conv_out, mixed_grad = (outputs[:, 0], outputs[:, 1])
    filt_grad = jnp.sum(outputs[:, 2].reshape(tok_rows, channels // groups, groups), axis=1)
    long_grad = lax.psum_scatter(filt_grad, "chan", scatter_dimension=1, tiled=True)
    feature_grad = jnp.stack(
        [upstream * conv_out, mixed_grad * value_rows, mixed_grad * key_rows], axis=0
    )
    upper_rim = shifted(feature_grad[:, : tap_count - 1, :], "seq", -1)
    trailing = jnp.concatenate([feature_grad, upper_rim], axis=1)
    input_grad = taps[:, 0, None, :] * feature_grad
    for lag_step in range(1, tap_count):
        input_grad = (
            input_grad + taps[:, lag_step, None, :] * trailing[:, lag_step : lag_step + tok_rows]
        )
    partial_taps = jnp.stack(
        [jnp.sum(feature_grad * lagged[lag_step], axis=1) for lag_step in range(tap_count)], axis=1
    )
    tap_grad = lax.psum(partial_taps, "seq") / math.sqrt(seq_width * tok_rows)
    return (input_grad.astype(jnp.bfloat16), long_grad, tap_grad)


def solution(mesh):
    return jax.shard_map(
        shards,
        mesh=mesh,
        in_specs=(P(None, "seq", "chan"), P(None, None, "chan"), P("seq", None), P("seq", "chan")),
        out_specs=(P(None, "seq", "chan"), P("seq", "chan"), P(None, None, "chan")),
        check_vma=False,
    )
```

profile of v0, /device:TPU:0, one launch (start us, length us, event | category | flops | bytes accessed | tf_op | source)
XLA Modules:
  0.0 260.5 jit_solution(12826561988551582519)
XLA Ops:
  8.0 4.9 %collective-permute-start = (bf16[3,2,1024]{2,1,0:T(2,128)(2,1)S(1)}, bf16[3,2,1024]{2,1,0:T(2,128)(2,1)S(1)}, u32[]{:S(2)}, u32[]{:S(2)}) collective-permute-start(bf16[3,2,1024]{2,1,0:T(2,128)(2,1)S(1)} %slice.70), channel_id=1, source_target_pairs={{0,4},{4,8},{8,12},{12,16},{16,20},{20,24},{24,28},{1,5},{5,9},{9,... | collective-permute-start | bytes 36872 | tf_op jit(solution)/shard_map/ppermute | solution.py:12
  14.4 2.3 copy.34
  20.7 2.0 maximum_convert_fusion
  22.7 3.2 %multiply_add_fusion = f32[3,128,1024]{1,2,0:T(8,128)S(1)} fusion(f32[3,130,1024]{1,2,0:T(8,128)S(1)} %maximum_convert_fusion, f32[3,1024]{1,0:T(4,128)S(1)} %get-tuple-element.26, f32[3,1024]{1,0:T(4,128)} %get-tuple-element.27, f32[3,1024]{1,0:T(4,128)S(1)} %bitcast.116), kind=kLoop, calls=%fused_computation.57 | loop fusion | flops 1966080 | bytes 6328320 | tf_op jit(solution)/shard_map/add | solution.py:91
  27.1 2.7 %pad_maximum_fusion.3 = f32[128,3,1024]{0,1,2:T(4,128)} fusion(f32[128,1,1024]{0,1,2:T(1,128)S(1)} %bitcast.113, f32[128,1,1024]{0,1,2:T(1,128)S(1)} %bitcast.114, f32[128,1,1024]{0,1,2:T(1,128)S(1)} %bitcast.112), kind=kLoop, calls=%fused_computation.33 | loop fusion | flops 786432 | bytes 3145728 | tf_op jit(solution)/shard_map/stack | solution.py:97
  29.8 4.9 %all-to-all-start = ((f32[128,3,1024]{0,1,2:T(4,128)}), f32[128,3,1024]{0,1,2:T(4,128)}, u32[]{:S(2)}, u32[]{:S(2)}) async-start(f32[128,3,1024]{0,1,2:T(4,128)} %pad_maximum_fusion.3), calls=%async_computation | async-start | bytes 4194304 | tf_op jit(solution)/shard_map/all_to_all | solution.py:33
  35.3 47.4 %all-to-all-done = f32[128,3,1024]{0,1,2:T(4,128)} async-done(((f32[128,3,1024]{0,1,2:T(4,128)}), f32[128,3,1024]{0,1,2:T(4,128)}, u32[]{:S(2)}, u32[]{:S(2)}) %all-to-all-start) | async-done | bytes 1572896 | tf_op jit(solution)/shard_map/all_to_all | solution.py:33
  82.7 5.1 %fusion.41 = f32[3,128,128,16]{2,3,1,0:T(8,128)S(1)} fusion(f32[128,3,8,128]{0,1,3,2:T(4,128)} %bitcast.5), kind=kOutput, calls=%fused_computation.45 | convolution fusion | flops 75499264 | bytes 4718592 | tf_op jit(solution)/shard_map/qm,ncmj->ncqj/dot_general | solution.py:22
  87.8 5.7 %fusion = (f32[3,128,16,128]{3,2,1,0:T(8,128)S(1)}, f32[3,128,16,128]{3,2,1,0:T(8,128)S(1)}) fusion(f32[3,128,128,16]{2,3,1,0:T(8,128)S(1)} %fusion.41, f32[16,128]{1,0:T(8,128)S(1)} %get-tuple-element.28, f32[16,128]{1,0:T(8,128)S(1)} %get-tuple-element.29, f32[128,3,8,128]{0,1,3,2:T(4,128)} %bitcast.5), kind=kOutput, calls=%fused_computation.5 | convolution fusion | flops 81004288 | bytes 11026432 | tf_op jit(solution)/shard_map/qm,ncmj->ncqj/dot_general | solution.py:22
  93.5 3.6 %fusion.18 = f32[3,128,16,128]{3,1,2,0:T(8,128)S(1)} fusion(f32[3,128,16,128]{3,2,1,0:T(8,128)S(1)} %get-tuple-element.13), kind=kOutput, calls=%fused_computation.25 | convolution fusion | flops 1208188928 | bytes 6291456 | tf_op jit(solution)/shard_map/rj,ncqj->ncqr/dot_general | solution.py:22
  97.2 3.9 %fusion.20 = f32[3,128,16,128]{3,1,2,0:T(8,128)S(1)} fusion(f32[3,128,16,128]{3,2,1,0:T(8,128)S(1)} %get-tuple-element.13), kind=kOutput, calls=%fused_computation.27 | convolution fusion | flops 1208188928 | bytes 6291456 | tf_op jit(solution)/shard_map/rj,ncqj->ncqr/dot_general | solution.py:22
  101.1 3.7 %fusion.29 = f32[3,128,16,128]{3,1,2,0:T(8,128)S(1)} fusion(f32[3,128,16,128]{3,1,2,0:T(8,128)S(1)} %fusion.18, f32[3,128,16,128]{3,2,1,0:T(8,128)S(1)} %get-tuple-element.12), kind=kOutput, calls=%fused_computation.35 | convolution fusion | flops 1208975360 | bytes 9437184 | tf_op jit(solution)/shard_map/rj,ncqj->ncqr/dot_general | solution.py:22
  104.7 3.7 %fusion.26 = f32[3,128,16,128]{3,1,2,0:T(8,128)S(1)} fusion(f32[3,128,16,128]{3,1,2,0:T(8,128)S(1)} %fusion.20, f32[3,128,16,128]{3,2,1,0:T(8,128)S(1)} %get-tuple-element.12), kind=kOutput, calls=%fused_computation.34 | convolution fusion | flops 1208975360 | bytes 9437184 | tf_op jit(solution)/shard_map/rj,ncqj->ncqr/dot_general | solution.py:22
  110.7 4.6 %fusion.10 = f32[3,128,16,128]{3,2,1,0:T(8,128)S(1)} fusion(f32[3,128,16,128]{3,1,2,0:T(8,128)S(1)} %pad_maximum_fusion.1), kind=kOutput, calls=%fused_computation.17 | convolution fusion | flops 1208188928 | bytes 6291456 | tf_op jit(solution)/shard_map/rj,ncqr->ncqj/dot_general | solution.py:22
  115.3 4.7 %fusion.12 = f32[3,128,16,128]{3,2,1,0:T(8,128)S(1)} fusion(f32[3,128,16,128]{3,1,2,0:T(8,128)S(1)} %pad_maximum_fusion.1), kind=kOutput, calls=%fused_computation.19 | convolution fusion | flops 1208188928 | bytes 6291456 | tf_op jit(solution)/shard_map/rj,ncqr->ncqj/dot_general | solution.py:22
  120.2 5.0 %fusion.35 = f32[3,128,16,128]{3,2,1,0:T(8,128)S(1)} fusion(f32[3,128,16,128]{3,2,1,0:T(8,128)S(1)} %fusion.10, f32[3,128,16,128]{3,1,2,0:T(8,128)S(1)} %pad_maximum_fusion), kind=kOutput, calls=%fused_computation.37 | convolution fusion | flops 1208975360 | bytes 9437184 | tf_op jit(solution)/shard_map/rj,ncqr->ncqj/dot_general | solution.py:22
  125.2 4.6 %fusion.32 = f32[3,128,16,128]{3,2,1,0:T(8,128)S(1)} fusion(f32[3,128,16,128]{3,2,1,0:T(8,128)S(1)} %fusion.12, f32[3,128,16,128]{3,1,2,0:T(8,128)S(1)} %pad_maximum_fusion), kind=kOutput, calls=%fused_computation.36 | convolution fusion | flops 1208975360 | bytes 9437184 | tf_op jit(solution)/shard_map/rj,ncqr->ncqj/dot_general | solution.py:22
  129.9 2.1 fusion.2
  132.0 3.4 %multiply_bitcast_fusion = f32[8,128,3,128]{1,0,3,2:T(8,128)} fusion(f32[3,128,128,8]{2,3,1,0:T(8,128)S(1)} %fusion.2, f32[3,128,16,128]{3,2,1,0:T(8,128)S(1)} %fusion.35, f32[3,128,16,128]{3,2,1,0:T(8,128)S(1)} %fusion.32, f32[16,128]{1,0:T(8,128)S(1)} %get-tuple-element.28, f32[16,128]{1,0:T(8,128)S(1)} %get-tuple-element.29), kind=kOutput, calls=%fused_computation.52 | convolution fusion | flops 78644992 | bytes 9453568 | tf_op jit(solution)/shard_map/mq,ncqj->ncmj/dot_general | solution.py:22
  135.3 3.5 %copy.67 = f32[8,128,3,128]{3,2,1,0:T(4,128)} copy(f32[8,128,3,128]{1,0,3,2:T(8,128)} %multiply_bitcast_fusion) | data formatting | bytes 3145728 | tf_op jit(solution)/shard_map/reshape | solution.py:69
  138.9 52.2 %all_to_all.30 = f32[1024,3,128]{2,1,0:T(4,128)} all-to-all(f32[1024,3,128]{2,1,0:T(4,128)} %bitcast.106), channel_id=1, replica_groups=mesh['seq'=8,'chan'=4] {'seq'}, dimensions={0} | all-to-all | bytes 3145728 | tf_op jit(solution)/shard_map/all_to_all | solution.py:71
  191.1 2.7 %copy.48 = f32[8,128,3,128]{1,3,0,2:T(8,128)} copy(f32[8,128,3,128]{3,2,1,0:T(4,128)} %bitcast.107) | data formatting | bytes 3145728 | tf_op jit(solution)/shard_map/all_to_all | solution.py:71
  193.8 1.4 fusion.55
  195.3 1.5 fusion.53
  198.1 1.9 copy.49
  201.2 1.9 slice.108
  203.1 1.7 reduce_sum.36
  205.7 1.7 copy.50
  207.3 2.2 pad_maximum_fusion.2
  209.6 5.2 %multiply_reduce_fusion.2 = (f32[3,1024]{1,0:T(4,128)S(1)}, f32[3,1024]{1,0:T(4,128)S(1)}, f32[3,1024]{1,0:T(4,128)S(1)}, bf16[3,128,1024]{1,2,0:T(8,128)(2,1)}) fusion(f32[3,130,1024]{1,2,0:T(8,128)S(1)} %maximum_convert_fusion, f32[1,128,1024]{1,2,0:T(8,128)S(1)} %copy-done.4, f32[1,128,1024]{1,2,0:T(8,128)S(1)} %copy-done.2, ...), kind=kLoop, calls=%fused_computation.51 | loop fusion | flops 5495808 | bytes 10297344 | tf_op jit(solution)/shard_map/reduce_sum | solution.py:126
  214.8 35.7 %psum.7 = f32[3,3,1024]{2,0,1:T(4,128)S(1)} all-reduce(f32[3,3,1024]{2,0,1:T(4,128)S(1)} %pad_maximum_fusion.5), channel_id=1, replica_groups=mesh['seq'=8,'chan'=4] {'seq'}, use_global_device_ids=true, to_apply=%region_5.6 | all-reduce | flops 9216 | bytes 73728 | tf_op jit(solution)/shard_map/psum | solution.py:128
  251.2 2.3 copy.51
  (45 shorter events, 14.8 us)
Async XLA Ops:
  8.0 11.5 %collective-permute-start = (bf16[3,2,1024]{2,1,0:T(2,128)(2,1)S(1)}, bf16[3,2,1024]{2,1,0:T(2,128)(2,1)S(1)}, u32[]{:S(2)}, u32[]{:S(2)}) collective-permute-start(bf16[3,2,1024]{2,1,0:T(2,128)(2,1)S(1)} %slice.70), channel_id=1, source_target_pairs={{0,4},{4,8},{8,12},{12,16},{16,20},{20,24},{24,28},{1,5},{5,9},{9,... | collective-permute-start | bytes 36872 | tf_op jit(solution)/shard_map/ppermute | solution.py:12
  20.7 2.0 copy-start.8
  25.8 1.2 copy-start
  29.8 52.9 %all-to-all-start = ((f32[128,3,1024]{0,1,2:T(4,128)}), f32[128,3,1024]{0,1,2:T(4,128)}, u32[]{:S(2)}, u32[]{:S(2)}) async-start(f32[128,3,1024]{0,1,2:T(4,128)} %pad_maximum_fusion.3), calls=%async_computation | async-start | bytes 4194304 | tf_op jit(solution)/shard_map/all_to_all | solution.py:33
  34.7 218.8 %reduce-scatter.2.cloned.1.call-start = ((), (), s32[]{:S(2)}) async-start(), calls=%async_computation.3 | async-start | bytes 163840 | tf_op jit(solution)/shard_map/reduce_scatter | solution.py:114
  195.3 1.5 copy-start.1
  195.3 2.8 %copy-start.3 = (f32[1,128,1024]{1,2,0:T(8,128)}, f32[1,128,1024]{1,2,0:T(8,128)S(1)}, u32[]{:S(2)}) copy-start(f32[1,128,1024]{1,2,0:T(8,128)S(1)} %get-tuple-element.21) | copy-start | bytes 1572868
  196.7 1.3 copy-start.5
  199.9 5.7 %collective-permute-start.1 = (f32[3,2,1024]{2,1,0:T(2,128)S(1)}, f32[3,2,1024]{2,1,0:T(2,128)S(1)}, u32[]{:S(2)}, u32[]{:S(2)}) collective-permute-start(f32[3,2,1024]{2,1,0:T(2,128)S(1)} %copy.49), channel_id=1, source_target_pairs={{4,0},{8,4},{12,8},{16,12},{20,16},{24,20},{28,24},{5,1},{9,5},{13... | collective-permute-start | bytes 73736 | tf_op jit(solution)/shard_map/ppermute | solution.py:12
  207.3 2.2 copy-start.2
  207.3 2.2 copy-start.4
  207.3 2.3 copy-start.6
  207.3 2.3 copy-start.7
  207.3 2.3 copy-start.9
Sparse Core Ops, SparseCore 0:
  205.0 19.6 reduce-scatter.1
where the time goes:
time: 265 us; the launch traced here: 261 us
  blocking collectives  87.9 us (33%)
  matrix products  50.1 us (19%)
  waiting for transfers between devices  48.2 us (18%)
  local copies, waits for them, and re-layouts  24.4 us (9%)
  other arithmetic  23.7 us (9%)
  between operations  14.5 us (5%)
  starting transfers between devices  11.6 us (4%)
    all_to_all x1, blocking collectives, whole_inverse(): lax.all_to_all(signal, 'seq', split_axis=0, concat_axis=2, tiled=True)  52.2 us
    dot_general x12, matrix products, contract(): jnp.einsum(pattern, factor_table, operand, precision=lax.Precision.HIGHEST)  50.1 us
    all_to_all x1, waiting for transfers between devices, whole_forward(): lax.all_to_all(signal, 'seq', split_axis=2, concat_axis=0, tiled=True)  47.4 us
    psum x1, blocking collectives, shards(): tap_grad = lax.psum(partial_taps, 'seq') / math.sqrt(seq_width * tok_rows)  35.7 us
    unnamed x27, local copies, waits for them, and re-layouts  9.76 us
    ppermute x2, starting transfers between devices, shifted(): return lax.ppermute(x, axis, pairs)  6.16 us
  transfers between devices with their start and end apart: 4, of which 2 were waited for; matrix products, arithmetic and copies ran while one was open for 9% of the time, Pallas kernels for 0%

commit v1 on v0

--- a/solution.py
+++ b/solution.py
@@ -1,9 +1,17 @@
+import functools
 import math
 
 import jax
 import jax.numpy as jnp
+import numpy as np
 from jax import lax
+from jax.experimental import pallas as pl
+from jax.experimental.pallas import tpu as pltpu
 from jax.sharding import PartitionSpec as P
+
+MESH = pl.DeviceIdType.MESH
+LANES = 128
+TABLE_LIMIT = 1024
 
 
 def shifted(x, axis, by):
@@ -129,9 +137,379 @@
     return (input_grad.astype(jnp.bfloat16), long_grad, tap_grad)
 
 
+def meet(axis_sizes):
+    barrier = pltpu.get_barrier_semaphore()
+    total = 0
+    for axis, size in axis_sizes:
+        me = lax.axis_index(axis)
+        for j in range(1, size):
+            pl.semaphore_signal(
+                barrier, inc=1, device_id={axis: lax.rem(me + j, size)}, device_id_type=MESH
+            )
+        total += size - 1
+    pl.semaphore_wait(barrier, total)
+
+
+def swap_matrix(reps, width):
+    side = reps * LANES
+    row = lax.broadcasted_iota(jnp.int32, (side, side), 0)
+    col = lax.broadcasted_iota(jnp.int32, (side, side), 1)
+    outer, inner, rest = row // LANES, (row % LANES) // width, row % width
+    hit = inner * LANES + outer * width + rest == col
+    return jnp.where(hit, 1.0, 0.0).astype(jnp.bfloat16)
+
+
+def lane_group(rows, width):
+    return lax.broadcasted_iota(jnp.int32, (rows, LANES), 1) // width
+
+
+def turn(x, shift, axis):
+    shift = shift % x.shape[axis]
+    return x if shift == 0 else pltpu.roll(x, shift, axis)
+
+
+def spread_kernel(n, reps, x_ref, og_ref, lf_ref, rb_ref, fr_ref, sb, fs, dsend, drecv, fsend, frecv):
+    me = lax.axis_index("seq")
+    width = LANES // reps
+    streams, rows, _ = x_ref.shape
+    meet([("seq", n)])
+    part = rows // reps
+    grp = lane_group(part, width)
+    for s in range(n):
+        base = (s // reps) * LANES
+        packed = jnp.zeros((part, LANES), jnp.float32)
+        for q in range(reps):
+            tile = lf_ref[q * part : (q + 1) * part, base : base + LANES]
+            packed = jnp.where(grp == q, turn(tile, (q - s % reps) * width, 1), packed)
+        fs[s] = packed
+    copies = []
+    for j in range(1, n):
+        peer = lax.rem(me + j, n)
+        copy = pltpu.make_async_remote_copy(
+            src_ref=fs.at[peer], dst_ref=fr_ref.at[me], send_sem=fsend.at[j - 1],
+            recv_sem=frecv.at[j - 1], device_id={"seq": peer}, device_id_type=MESH,
+        )
+        copy.start()
+        copies.append(copy)
+    swap = swap_matrix(reps, width)
+    tiles = n // reps
+    for h in range(tiles):
+        for p in range(streams + 1):
+            source = x_ref.at[p] if p < streams else og_ref
+            joined = jnp.concatenate(
+                [source[:, (r * tiles + h) * LANES : (r * tiles + h + 1) * LANES] for r in range(reps)],
+                axis=1,
+            )
+            moved = jnp.dot(joined, swap, preferred_element_type=jnp.float32).astype(jnp.bfloat16)
+            for g in range(reps):
+                sb[h * reps + g, p] = moved[:, g * LANES : (g + 1) * LANES]
+    for j in range(1, n):
+        peer = lax.rem(me + j, n)
+        copy = pltpu.make_async_remote_copy(
+            src_ref=sb.at[peer], dst_ref=rb_ref.at[me], send_sem=dsend.at[j - 1],
+            recv_sem=drecv.at[j - 1], device_id={"seq": peer}, device_id_type=MESH,
+        )
+        copy.start()
+        copies.append(copy)
+    rb_ref[me] = sb[me]
+    fr_ref[me] = fs[me]
+    for copy in copies:
+        copy.wait()
+
+
+def halves(x):
+    high = x.astype(jnp.bfloat16)
+    return high, (x - high.astype(jnp.float32)).astype(jnp.bfloat16)
+
+
+def later(x, lag):
+    if lag == 0:
+        return x
+    row = lax.broadcasted_iota(jnp.int32, x.shape, 0)
+    return jnp.where(row < lag, 0.0, pltpu.roll(x, lag, 0))
+
+
+def sooner(x, lag):
+    if lag == 0:
+        return x
+    row = lax.broadcasted_iota(jnp.int32, x.shape, 0)
+    return jnp.where(row >= x.shape[0] - lag, 0.0, pltpu.roll(x, x.shape[0] - lag, 0))
+
+
+def group_sum(x, reps):
+    total = x
+    for r in range(1, reps):
+        total = total + turn(x, r * (LANES // reps), 1)
+    return total
+
+
+def three(high, low, x_high, x_low):
+    def dot(a, b):
+        return jnp.dot(a, b, preferred_element_type=jnp.float32)
+
+    return dot(high, x_high) + (dot(high, x_low) + dot(low, x_high))
+
+
+def make_table(ca, sa, cb, sb, ch, cl, sh, sl):
+    step = cb.shape[0]
+
+    @pl.loop(0, ca.shape[0])
+    def _(i):
+        c0, s0 = ca[pl.ds(i, 1), :], sa[pl.ds(i, 1), :]
+        rows = pl.ds(pl.multiple_of(i * step, step), step)
+        ch[rows, :], cl[rows, :] = halves(c0 * cb[...] - s0 * sb[...])
+        sh[rows, :], sl[rows, :] = halves(s0 * cb[...] + c0 * sb[...])
+
+
+def layer_kernel(
+    n, reps, rb_ref, fr_ref, tp_ref, ca, sa, cb, sb, ig_ref, lg_ref, tg_ref,
+    ch, cl, sh, sl, xh, xl, ah, al, bh, bl, res,
+):
+    me = lax.axis_index("seq")
+    rows = rb_ref.shape[2]
+    tokens = n * rows
+    width = LANES // reps
+    part = rows // reps
+    taps = tp_ref[me]
+    tap_count = 3
+    make_table(ca, sa, cb, sb, ch, cl, sh, sl)
+
+    def stream(p):
+        return rb_ref[:, p].reshape(tokens, LANES).astype(jnp.float32)
+
+    def feature(p):
+        x = stream(p)
+        total = taps[tap_count * p][None, :] * x
+        for lag in range(1, tap_count):
+            total = total + taps[tap_count * p + lag][None, :] * later(x, lag)
+        return total
+
+    def alternating(count):
+        row = lax.broadcasted_iota(jnp.int32, (count, LANES), 0)
+        return jnp.where(row % 2 == 0, 1.0, -1.0)
+
+    sign = alternating(tokens)
+    mixed = feature(1) * feature(2)
+    xh[:, :LANES], xl[:, :LANES] = halves(mixed)
+    mixed_end = jnp.sum(sign * mixed, axis=0, keepdims=True)
+    grad = stream(3) * feature(0)
+    xh[:, LANES : 2 * LANES], xl[:, LANES : 2 * LANES] = halves(grad)
+    grad_end = jnp.sum(sign * grad, axis=0, keepdims=True)
+    grp = lane_group(part, width)
+    filt_end = jnp.zeros((1, LANES), jnp.float32)
+    for s in range(n):
+        packed = fr_ref[s]
+        for q in range(reps):
+            piece = group_sum(jnp.where(grp == q, packed, 0.0), reps)
+            filt_end = filt_end + jnp.sum(alternating(part) * piece, axis=0, keepdims=True)
+            at = s * rows + q * part
+            xh[at : at + part, 2 * LANES :], xl[at : at + part, 2 * LANES :] = halves(piece)
+    chunk = min(256, tokens)
+
+    @pl.loop(0, tokens // chunk)
+    def _(i):
+        at = pl.ds(pl.multiple_of(i * chunk, chunk), chunk)
+        a = three(ch[at, :], cl[at, :], xh[...], xl[...])
+        b = three(sh[at, :], sl[at, :], xh[...], xl[...])
+        am, ag, af = (a[:, k * LANES : (k + 1) * LANES] for k in range(3))
+        bm, bg, bf = (b[:, k * LANES : (k + 1) * LANES] for k in range(3))
+        row = lax.broadcasted_iota(jnp.int32, (chunk, LANES), 0) + i * chunk
+        weight = jnp.where(row == 0, 0.5 / tokens, 1.0 / tokens)
+        evens = (af * am - bf * bm, af * ag + bf * bg, group_sum(ag * am + bg * bm, reps))
+        odds = (af * bm + bf * am, af * bg - bf * ag, group_sum(bg * am - ag * bm, reps))
+        for k in range(3):
+            lanes = slice(k * LANES, (k + 1) * LANES)
+            ah[at, lanes], al[at, lanes] = halves(evens[k] * weight)
+            bh[at, lanes], bl[at, lanes] = halves(odds[k] * weight)
+
+    ends = jnp.concatenate(
+        [filt_end * mixed_end, filt_end * grad_end, group_sum(grad_end * mixed_end, reps)], axis=1
+    ) * (0.5 / tokens)
+
+    @pl.loop(0, tokens // chunk)
+    def _(i):
+        at = pl.ds(pl.multiple_of(i * chunk, chunk), chunk)
+        total = three(ch[at, :], cl[at, :], ah[...], al[...])
+        total = total + three(sh[at, :], sl[at, :], bh[...], bl[...])
+        row = lax.broadcasted_iota(jnp.int32, total.shape, 0)
+        res[at, :] = total + jnp.where(row % 2 == 0, ends, -ends)
+
+    for s in range(n):
+        packed = jnp.zeros((part, LANES), jnp.float32)
+        for q in range(reps):
+            at = s * rows + q * part
+            packed = jnp.where(grp == q, res[at : at + part, 2 * LANES :], packed)
+        lg_ref[s] = packed
+    for p in range(3):
+        if p == 0:
+            grads = stream(3) * res[:, :LANES]
+        else:
+            grads = res[:, LANES : 2 * LANES] * feature(3 - p)
+        x = stream(p)
+        total = taps[tap_count * p][None, :] * grads
+        for lag in range(tap_count):
+            line = jnp.sum(grads * later(x, lag), axis=0, keepdims=True)
+            tg_ref[tap_count * p + lag : tap_count * p + lag + 1, :] = line * (1.0 / math.sqrt(tokens))
+            if lag > 0:
+                total = total + taps[tap_count * p + lag][None, :] * sooner(grads, lag)
+        ig_ref[:, p] = total.astype(jnp.bfloat16).reshape(n, rows, LANES)
+
+
+def collect_kernel(
+    n, m, reps, ig_ref, lg_ref, tg_ref, out_ref, lo_ref, to_ref,
+    ir, lr, l2, isend, irecv, lsend, lrecv, tsend, trecv, csend, crecv,
+):
+    me, mine = lax.axis_index("seq"), lax.axis_index("chan")
+    meet([("seq", n), ("chan", m)])
+    firsts, rest = [], []
+    for j in range(1, n):
+        peer = lax.rem(me + j, n)
+        copy = pltpu.make_async_remote_copy(
+            src_ref=lg_ref.at[peer], dst_ref=lr.at[me], send_sem=lsend.at[j - 1],
+            recv_sem=lrecv.at[j - 1], device_id={"seq": peer}, device_id_type=MESH,
+        )
+        copy.start()
+        firsts.append(copy)
+    for j in range(1, n):
+        peer = lax.rem(me + j, n)
+        for src, dst, send, recv in (
+            (ig_ref.at[peer], ir.at[me], isend, irecv), (tg_ref, to_ref.at[me], tsend, trecv)
+        ):
+            copy = pltpu.make_async_remote_copy(
+                src_ref=src, dst_ref=dst, send_sem=send.at[j - 1],
+                recv_sem=recv.at[j - 1], device_id={"seq": peer}, device_id_type=MESH,
+            )
+            copy.start()
+            rest.append(copy)
+    lr[me] = lg_ref[me]
+    ir[me] = ig_ref[me]
+    to_ref[me] = tg_ref[...]
+    swap = swap_matrix(reps, LANES // reps)
+    for copy in firsts:
+        copy.wait()
+    per = n // m
+    seconds = []
+    for j in range(1, m):
+        peer = lax.rem(mine + j, m)
+        copy = pltpu.make_async_remote_copy(
+            src_ref=lr.at[pl.ds(peer * per, per)], dst_ref=l2.at[mine], send_sem=csend.at[j - 1],
+            recv_sem=crecv.at[j - 1], device_id={"chan": peer}, device_id_type=MESH,
+        )
+        copy.start()
+        seconds.append(copy)
+    l2[mine] = lr[pl.ds(mine * per, per)]
+    for copy in rest + seconds:
+        copy.wait()
+    total = l2[0]
+    for k in range(1, m):
+        total = total + l2[k]
+    lo_ref[...] = total
+    tiles = n // reps
+    for h in range(tiles):
+        for p in range(3):
+            joined = jnp.concatenate([ir[h * reps + g, p] for g in range(reps)], axis=1)
+            moved = jnp.dot(joined, swap, preferred_element_type=jnp.float32).astype(jnp.bfloat16)
+            for r in range(reps):
+                at = (r * tiles + h) * LANES
+                out_ref[p, :, at : at + LANES] = moved[:, r * LANES : (r + 1) * LANES]
+
+
+def dma(count):
+    return pltpu.SemaphoreType.DMA((count,))
+
+
+def whole_specs(count):
+    return [pl.BlockSpec(memory_space=pltpu.VMEM)] * count
+
+
+def params(which=None):
+    if which is None:
+        return pltpu.CompilerParams(vmem_limit_bytes=56 << 20)
+    return pltpu.CompilerParams(collective_id=which, has_side_effects=True, vmem_limit_bytes=32 << 20)
+
+
+def half_tables(tokens):
+    step = 32
+    col = np.arange(tokens)
+    coarse = np.arange(tokens // step)[:, None] * step * col[None, :] % (2 * tokens)
+    fine = np.arange(step)[:, None] * col[None, :] % (2 * tokens)
+    out = []
+    for index in (coarse, fine):
+        phase = index * (math.pi / tokens)
+        out += [np.cos(phase).astype(np.float32), np.sin(phase).astype(np.float32)]
+    return out
+
+
+def fast_shards(n, m, proj_in, taps, long_filter, out_grad):
+    streams, rows, channels = proj_in.shape
+    groups = long_filter.shape[1]
+    reps = channels // groups
+    width = groups // n
+    part = rows // reps
+    tokens = n * rows
+    f32, bf16 = jnp.float32, jnp.bfloat16
+    shape = jax.ShapeDtypeStruct
+    lined = taps.reshape(streams * 3, reps, n, width).transpose(2, 0, 1, 3).reshape(n, -1, LANES)
+    lined = jnp.pad(lined, ((0, 0), (0, 16 - streams * 3), (0, 0)))
+    rb, fr = pl.pallas_call(
+        functools.partial(spread_kernel, n, reps),
+        out_shape=(shape((n, streams + 1, rows, LANES), bf16), shape((n, part, LANES), f32)),
+        in_specs=whole_specs(3),
+        out_specs=whole_specs(2),
+        scratch_shapes=[
+            pltpu.VMEM((n, streams + 1, rows, LANES), bf16), pltpu.VMEM((n, part, LANES), f32),
+        ] + [dma(n - 1)] * 4,
+        compiler_params=params(0),
+    )(proj_in, out_grad, long_filter)
+    ca, sa, cb, sb = half_tables(tokens)
+    side = pltpu.VMEM((tokens, tokens), bf16)
+    tall = pltpu.VMEM((tokens, 3 * LANES), bf16)
+    ig, lg, tg = pl.pallas_call(
+        functools.partial(layer_kernel, n, reps),
+        out_shape=(
+            shape((n, streams, rows, LANES), bf16), shape((n, part, LANES), f32), shape((16, LANES), f32),
+        ),
+        in_specs=whole_specs(7),
+        out_specs=whole_specs(3),
+        scratch_shapes=[side] * 4 + [tall] * 6 + [pltpu.VMEM((tokens, 3 * LANES), f32)],
+        compiler_params=params(),
+    )(rb, fr, lined, ca, sa, cb, sb)
+    out, lo, to = pl.pallas_call(
+        functools.partial(collect_kernel, n, m, reps),
+        out_shape=(
+            shape((streams, rows, channels), bf16), shape((n // m, part, LANES), f32), shape((n, 16, LANES), f32),
+        ),
+        in_specs=whole_specs(3),
+        out_specs=whole_specs(3),
+        scratch_shapes=[
+            pltpu.VMEM((n, streams, rows, LANES), bf16), pltpu.VMEM((n, part, LANES), f32),
+            pltpu.VMEM((m, n // m, part, LANES), f32),
+        ] + [dma(n - 1)] * 6 + [dma(m - 1)] * 2,
+        compiler_params=params(1),
+    )(ig, lg, tg)
+    long_grad = lo.reshape(n // m, part, reps, width).transpose(2, 1, 0, 3).reshape(rows, groups // m)
+    tap_grad = to[:, : streams * 3].reshape(n, streams * 3, reps, width).transpose(1, 2, 0, 3)
+    return (out, long_grad, tap_grad.reshape(streams, 3, channels))
+
+
+def fits(n, m, proj_in, taps, long_filter, out_grad):
+    streams, rows, channels = proj_in.shape
+    groups = long_filter.shape[1]
+    if channels % groups or groups % n or n % m or streams != 3 or taps.shape[1] != 3:
+        return False
+    reps, width = channels // groups, groups // n
+    if reps < 2 or reps * width != LANES or n % reps or rows % (8 * reps) or rows % 16:
+        return False
+    return n * rows <= TABLE_LIMIT and n * rows % 256 == 0
+
+
+def routed(n, m, *arrays):
+    return fast_shards(n, m, *arrays) if fits(n, m, *arrays) else shards(*arrays)
+
+
 def solution(mesh):
     return jax.shard_map(
-        shards,
+        functools.partial(routed, mesh.shape["seq"], mesh.shape["chan"]),
         mesh=mesh,
         in_specs=(P(None, "seq", "chan"), P(None, None, "chan"), P("seq", None), P("seq", "chan")),
         out_specs=(P(None, "seq", "chan"), P("seq", "chan"), P(None, None, "chan")),

time: 265 us -> 91.5 us (0.35)
  the two profiles are of different devices: /device:TPU:0 before, /device:TPU:12 now
where the time goes in v1:
time: 91.5 us; the launch traced here: 91.2 us
  Pallas kernels  79.8 us (87%)
  local copies, waits for them, and re-layouts  10.7 us (12%)
    pallas_call x1, Pallas kernels, fast_shards(): pl.pallas_call(functools.partial(spread_kernel, n, reps), out_shape=(shap...  30.2 us
    pallas_call x1, Pallas kernels, fast_shards(): pl.pallas_call(functools.partial(collect_kernel, n, m, reps), out_shape=(...  25.7 us
    pallas_call x1, Pallas kernels, fast_shards(): pl.pallas_call(functools.partial(layer_kernel, n, reps), out_shape=(shape...  23.9 us
    unnamed x17, local copies, waits for them, and re-layouts  7.09 us

profile of v1, /device:TPU:12, one launch (start us, length us, event | category | flops | bytes accessed | tf_op | source)
XLA Modules:
  0.0 91.2 jit_solution(12270561367511573437)
XLA Ops:
  0.6 0.0 copy-start.1
  0.6 1.0 %reshape.24 = f32[9,4,8,32]{3,2,1,0:T(8,128)S(1)} reshape(f32[3,3,1024]{2,1,0:T(4,128)} %param.9) | data formatting | bytes 73728 | tf_op jit(solution)/shard_map/reshape | solution.py:452
  1.7 0.1 reshape.25
  1.8 0.6 pad.4.tp_ref
  2.4 0.0 copy-done.1
  2.5 0.0 copy-start.3
  2.5 0.9 %copy-done.3 = bf16[128,1024]{1,0:T(8,128)(2,1)S(1)} copy-done((bf16[128,1024]{1,0:T(8,128)(2,1)S(1)}, bf16[128,1024]{1,0:T(8,128)(2,1)}, u32[]{:S(2)}) %copy-start.3) | copy-done | bytes 262168
  3.4 0.0 copy-start.4
  3.4 0.9 copy-done.4
  4.3 30.2 %shard_map.103 = (bf16[8,4,128,128]{3,2,1,0:T(8,128)(2,1)S(1)}, f32[8,32,128]{2,1,0:T(8,128)S(1)}) custom-call(bf16[3,128,1024]{2,1,0:T(8,128)(2,1)S(1)} %copy-done.1, bf16[128,1024]{1,0:T(8,128)(2,1)S(1)} %copy-done.3, f32[128,256]{1,0:T(8,128)S(1)} %copy-done.4), custom_call_target="tpu_custom_call" | custom-call | tf_op jit(solution)/shard_map/pallas_call | solution.py:454
  34.5 0.0 copy-start
  34.5 1.0 %copy-done = bf16[8,4,128,128]{3,2,1,0:T(8,128)(2,1)} copy-done((bf16[8,4,128,128]{3,2,1,0:T(8,128)(2,1)}, bf16[8,4,128,128]{3,2,1,0:T(8,128)(2,1)S(1)}, u32[]{:S(2)}) %copy-start) | copy-done | bytes 1048600
  35.5 0.0 copy-start.6
  35.5 0.7 copy-done.6
  36.1 23.9 %shard_map.104 = (bf16[8,3,128,128]{3,2,1,0:T(8,128)(2,1)}, f32[8,32,128]{2,1,0:T(8,128)}, f32[16,128]{1,0:T(8,128)}) custom-call(bf16[8,4,128,128]{3,2,1,0:T(8,128)(2,1)} %copy-done, f32[8,32,128]{2,1,0:T(8,128)} %copy-done.6, f32[8,16,128]{2,1,0:T(8,128)} %pad.4.tp_ref, f32[32,1024]{1,0:T(8,128)} %constant.11.clone.ca, f32[32,1024]{1,0:T(8,128)} %constant.12.clone.sa, ...), custom_call_target="tpu_custom_call" | custom-call | tf_op jit(solution)/shard_map/pallas_call | solution.py:467
  60.0 0.0 copy-start.2
  60.0 1.1 %copy-done.2 = bf16[8,3,128,128]{3,2,1,0:T(8,128)(2,1)S(1)} copy-done((bf16[8,3,128,128]{3,2,1,0:T(8,128)(2,1)S(1)}, bf16[8,3,128,128]{3,2,1,0:T(8,128)(2,1)}, u32[]{:S(2)}) %copy-start.2) | copy-done | bytes 786456
  61.2 0.0 copy-start.5
  61.2 0.9 copy-done.5
  62.1 0.0 copy-start.7
  62.1 0.7 copy-done.7
  62.8 25.7 %shard_map.105 = (bf16[3,128,1024]{2,1,0:T(8,128)(2,1)S(1)}, f32[2,32,128]{2,1,0:T(8,128)S(1)}, f32[8,16,128]{2,1,0:T(8,128)S(1)}) custom-call(bf16[8,3,128,128]{3,2,1,0:T(8,128)(2,1)S(1)} %copy-done.2, f32[8,32,128]{2,1,0:T(8,128)S(1)} %copy-done.5, f32[16,128]{1,0:T(8,128)S(1)} %copy-done.7), custom_call_target="tpu_custom_call" | custom-call | tf_op jit(solution)/shard_map/pallas_call | solution.py:477
  88.5 0.1 reshape.28
  88.6 0.7 reshape.29
  89.4 0.1 reshape.26
  89.5 0.1 copy.20
  89.6 0.7 reshape.27
  90.4 0.9 copy.26
  (4 shorter events, 0.1 us)
Async XLA Ops:
  0.6 1.8 %copy-start.1 = (bf16[3,128,1024]{2,1,0:T(8,128)(2,1)S(1)}, bf16[3,128,1024]{2,1,0:T(8,128)(2,1)}, u32[]{:S(2)}) copy-start(bf16[3,128,1024]{2,1,0:T(8,128)(2,1)} %x_ref.1) | copy-start | bytes 2359300
  2.5 1.0 %copy-start.3 = (bf16[128,1024]{1,0:T(8,128)(2,1)S(1)}, bf16[128,1024]{1,0:T(8,128)(2,1)}, u32[]{:S(2)}) copy-start(bf16[128,1024]{1,0:T(8,128)(2,1)} %og_ref.1) | copy-start | bytes 786436
  3.4 0.9 copy-start.4
  34.5 1.0 %copy-start = (bf16[8,4,128,128]{3,2,1,0:T(8,128)(2,1)}, bf16[8,4,128,128]{3,2,1,0:T(8,128)(2,1)S(1)}, u32[]{:S(2)}) copy-start(bf16[8,4,128,128]{3,2,1,0:T(8,128)(2,1)S(1)} %get-tuple-element.11.rb_ref) | copy-start | bytes 3145732
  35.5 0.7 copy-start.6
  60.0 1.1 %copy-start.2 = (bf16[8,3,128,128]{3,2,1,0:T(8,128)(2,1)S(1)}, bf16[8,3,128,128]{3,2,1,0:T(8,128)(2,1)}, u32[]{:S(2)}) copy-start(bf16[8,3,128,128]{3,2,1,0:T(8,128)(2,1)} %get-tuple-element.13.ig_ref) | copy-start | bytes 2359300
  61.2 0.9 copy-start.5
  62.1 0.7 copy-start.7

commit v2 on v0

--- a/solution.py
+++ b/solution.py
@@ -1,9 +1,17 @@
+import functools
 import math
 
 import jax
 import jax.numpy as jnp
+import numpy as np
 from jax import lax
+from jax.experimental import pallas as pl
+from jax.experimental.pallas import tpu as pltpu
 from jax.sharding import PartitionSpec as P
+
+MESH = pl.DeviceIdType.MESH
+LANES = 128
+TABLE_LIMIT = 1024
 
 
 def shifted(x, axis, by):
@@ -129,9 +137,403 @@
     return (input_grad.astype(jnp.bfloat16), long_grad, tap_grad)
 
 
+def meet(axis_sizes):
+    barrier = pltpu.get_barrier_semaphore()
+    total = 0
+    for axis, size in axis_sizes:
+        me = lax.axis_index(axis)
+        for j in range(1, size):
+            pl.semaphore_signal(
+                barrier, inc=1, device_id={axis: lax.rem(me + j, size)}, device_id_type=MESH
+            )
+        total += size - 1
+    pl.semaphore_wait(barrier, total)
+
+
+def swap_matrix(reps, width):
+    side = reps * LANES
+    row = lax.broadcasted_iota(jnp.int32, (side, side), 0)
+    col = lax.broadcasted_iota(jnp.int32, (side, side), 1)
+    outer, inner, rest = row // LANES, (row % LANES) // width, row % width
+    hit = inner * LANES + outer * width + rest == col
+    return jnp.where(hit, 1.0, 0.0).astype(jnp.bfloat16)
+
+
+def lane_group(rows, width):
+    return lax.broadcasted_iota(jnp.int32, (rows, LANES), 1) // width
+
+
+def turn(x, shift, axis):
+    shift = shift % x.shape[axis]
+    return x if shift == 0 else pltpu.roll(x, shift, axis)
+
+
+def halves(x):
+    high = x.astype(jnp.bfloat16)
+    return high, (x - high.astype(jnp.float32)).astype(jnp.bfloat16)
+
+
+def later(x, lag):
+    if lag == 0:
+        return x
+    row = lax.broadcasted_iota(jnp.int32, x.shape, 0)
+    return jnp.where(row < lag, 0.0, pltpu.roll(x, lag, 0))
+
+
+def sooner(x, lag):
+    if lag == 0:
+        return x
+    row = lax.broadcasted_iota(jnp.int32, x.shape, 0)
+    return jnp.where(row >= x.shape[0] - lag, 0.0, pltpu.roll(x, x.shape[0] - lag, 0))
+
+
+def group_sum(x, reps):
+    total = x
+    for r in range(1, reps):
+        total = total + turn(x, r * (LANES // reps), 1)
+    return total
+
+
+def three(high, low, x_high, x_low):
+    def dot(a, b):
+        return jnp.dot(a, b, preferred_element_type=jnp.float32)
+
+    return dot(high, x_high) + (dot(high, x_low) + dot(low, x_high))
+
+
+def make_table(ca, sa, cb, sb, ch, cl, sh, sl):
+    step = cb.shape[0]
+
+    @pl.loop(0, ca.shape[0])
+    def _(i):
+        c0, s0 = ca[pl.ds(i, 1), :], sa[pl.ds(i, 1), :]
+        rows = pl.ds(pl.multiple_of(i * step, step), step)
+        ch[rows, :], cl[rows, :] = halves(c0 * cb[...] - s0 * sb[...])
+        sh[rows, :], sl[rows, :] = halves(s0 * cb[...] + c0 * sb[...])
+
+
+def whole_kernel(
+    n, m, reps, x_ref, og_ref, lf_ref, tp_ref, ca, sa, cb, sb, out_ref, lo_ref, to_ref,
+    xs, xr, fs, fr, ch, cl, sh, sl, mh, ml, gg, sa_f, sb_f, eh, el, oh, ol, ec, oc, res, res0,
+    igs, igr, lgs, lgr, l2, tgs, tgr, sems, csems,
+):
+    me, mine = lax.axis_index("seq"), lax.axis_index("chan")
+    width = LANES // reps
+    streams, rows, _ = x_ref.shape
+    tap_count = tp_ref.shape[1]
+    tokens = n * rows
+    part = rows // reps
+    tiles = n // reps
+    meet([("seq", n), ("chan", m)])
+    grp = lane_group(part, width)
+
+    def ship(kind, source, target):
+        copies = []
+        for j in range(1, n):
+            peer = lax.rem(me + j, n)
+            copy = pltpu.make_async_remote_copy(
+                src_ref=source(peer), dst_ref=target, send_sem=sems.at[0, kind, j - 1],
+                recv_sem=sems.at[1, kind, j - 1], device_id={"seq": peer}, device_id_type=MESH,
+            )
+            copy.start()
+            copies.append(copy)
+        return copies
+
+    swap = swap_matrix(reps, width)
+
+    def gather_stream(source, place):
+        for h in range(tiles):
+            joined = jnp.concatenate(
+                [source[:, (r * tiles + h) * LANES : (r * tiles + h + 1) * LANES] for r in range(reps)],
+                axis=1,
+            )
+            moved = jnp.dot(joined, swap, preferred_element_type=jnp.float32).astype(jnp.bfloat16)
+            for g in range(reps):
+                xs[place // 2, h * reps + g, place % 2] = moved[:, g * LANES : (g + 1) * LANES]
+
+    gather_stream(x_ref.at[1], 0)
+    gather_stream(x_ref.at[2], 1)
+    first = ship(0, lambda peer: xs.at[0, peer], xr.at[0, me])
+    for s in range(n):
+        base = (s // reps) * LANES
+        packed = jnp.zeros((part, LANES), jnp.float32)
+        for q in range(reps):
+            tile = lf_ref[q * part : (q + 1) * part, base : base + LANES]
+            packed = jnp.where(grp == q, turn(tile, (q - s % reps) * width, 1), packed)
+        fs[s] = packed
+    first += ship(1, lambda peer: fs.at[peer], fr.at[me])
+    gather_stream(x_ref.at[0], 2)
+    gather_stream(og_ref, 3)
+    second = ship(2, lambda peer: xs.at[1, peer], xr.at[1, me])
+    xr[0, me] = xs[0, me]
+    xr[1, me] = xs[1, me]
+    fr[me] = fs[me]
+
+    taps = []
+    home, slot = me // reps, lax.rem(me, reps)
+    for p in range(streams):
+        mixed_taps = jnp.zeros((tap_count, LANES), jnp.float32)
+        for r in range(reps):
+            at = pl.multiple_of((r * tiles + home) * LANES, LANES)
+            tile = tp_ref[p, :, pl.ds(at, LANES)]
+            shift = lax.rem((r + reps - slot) * width, LANES)
+            mixed_taps = jnp.where(
+                lane_group(tap_count, width) == r, pltpu.roll(tile, shift, 1), mixed_taps
+            )
+        taps.append([mixed_taps[i : i + 1] for i in range(tap_count)])
+    tgs[...] = jnp.zeros_like(tgs)
+    make_table(ca, sa, cb, sb, ch, cl, sh, sl)
+
+    places = {1: (0, 0), 2: (0, 1), 0: (1, 0), 3: (1, 1)}
+
+    def stream(p):
+        half, at = places[p]
+        return xr[half, :, at].reshape(tokens, LANES).astype(jnp.float32)
+
+    def feature(p):
+        x = stream(p)
+        total = taps[p][0] * x
+        for lag in range(1, tap_count):
+            total = total + taps[p][lag] * later(x, lag)
+        return total
+
+    def alternating(count):
+        row = lax.broadcasted_iota(jnp.int32, (count, LANES), 0)
+        return jnp.where(row % 2 == 0, 1.0, -1.0)
+
+    def dot(left, right):
+        return jnp.dot(left, right, preferred_element_type=jnp.float32)
+
+    def paired(high, low, both):
+        wide = dot(high, both[...])
+        return wide[:, :LANES] + (wide[:, LANES:] + dot(low, both[:, :LANES]))
+
+    def weight_of(i, count):
+        row = lax.broadcasted_iota(jnp.int32, (count, LANES), 0) + i * count
+        return jnp.where(row == 0, 0.5 / tokens, 1.0 / tokens)
+
+    for copy in first:
+        copy.wait()
+    sign = alternating(tokens)
+    mixed = feature(1) * feature(2)
+    mh[:, :LANES], ml[:, :LANES] = halves(mixed)
+    mixed_end = jnp.sum(sign * mixed, axis=0, keepdims=True)
+    filt_end = jnp.zeros((1, LANES), jnp.float32)
+    for s in range(n):
+        packed = fr[s]
+        for q in range(reps):
+            piece = group_sum(jnp.where(grp == q, packed, 0.0), reps)
+            filt_end = filt_end + jnp.sum(alternating(part) * piece, axis=0, keepdims=True)
+            at = s * rows + q * part
+            mh[at : at + part, LANES:], ml[at : at + part, LANES:] = halves(piece)
+    chunk = min(256, tokens)
+
+    @pl.loop(0, tokens // chunk)
+    def _(i):
+        at = pl.ds(pl.multiple_of(i * chunk, chunk), chunk)
+        a = three(ch[at, :], cl[at, :], mh[...], ml[...])
+        b = three(sh[at, :], sl[at, :], mh[...], ml[...])
+        sa_f[at, :], sb_f[at, :] = a, b
+        am, af, bm, bf = a[:, :LANES], a[:, LANES:], b[:, :LANES], b[:, LANES:]
+        weight = weight_of(i, chunk)
+        ec[at, :LANES], ec[at, LANES:] = halves((af * am - bf * bm) * weight)
+        oc[at, :LANES], oc[at, LANES:] = halves((af * bm + bf * am) * weight)
+
+    for copy in second:
+        copy.wait()
+    grad = stream(3) * feature(0)
+    gg[:, :LANES], gg[:, LANES:] = halves(grad)
+    grad_end = jnp.sum(sign * grad, axis=0, keepdims=True)
+
+    @pl.loop(0, tokens // chunk)
+    def _(i):
+        at = pl.ds(pl.multiple_of(i * chunk, chunk), chunk)
+        ag = paired(ch[at, :], cl[at, :], gg)
+        bg = paired(sh[at, :], sl[at, :], gg)
+        am, af, bm, bf = sa_f[at, :LANES], sa_f[at, LANES:], sb_f[at, :LANES], sb_f[at, LANES:]
+        weight = weight_of(i, chunk)
+        eh[at, :LANES], el[at, :LANES] = halves((af * ag + bf * bg) * weight)
+        oh[at, :LANES], ol[at, :LANES] = halves((af * bg - bf * ag) * weight)
+        eh[at, LANES:], el[at, LANES:] = halves(group_sum(ag * am + bg * bm, reps) * weight)
+        oh[at, LANES:], ol[at, LANES:] = halves(group_sum(bg * am - ag * bm, reps) * weight)
+
+    ends = jnp.concatenate(
+        [filt_end * grad_end, group_sum(grad_end * mixed_end, reps)], axis=1
+    ) * (0.5 / tokens)
+    conv_end = filt_end * mixed_end * (0.5 / tokens)
+
+    @pl.loop(0, tokens // chunk)
+    def _(i):
+        at = pl.ds(pl.multiple_of(i * chunk, chunk), chunk)
+        total = three(ch[at, :], cl[at, :], eh[...], el[...])
+        total = total + three(sh[at, :], sl[at, :], oh[...], ol[...])
+        row = lax.broadcasted_iota(jnp.int32, total.shape, 0)
+        res[at, :] = total + jnp.where(row % 2 == 0, ends, -ends)
+
+    def finish(p, grads, place):
+        total = taps[p][0] * grads
+        for lag in range(1, tap_count):
+            total = total + taps[p][lag] * sooner(grads, lag)
+        place[...] = total.astype(jnp.bfloat16).reshape(n, rows, LANES)
+
+    def tap_lines(p, grads):
+        x = stream(p)
+        for lag in range(tap_count):
+            line = jnp.sum(grads * later(x, lag), axis=0, keepdims=True)
+            tgs[tap_count * p + lag : tap_count * p + lag + 1, :] = line * (1.0 / math.sqrt(tokens))
+
+    for s in range(n):
+        packed = jnp.zeros((part, LANES), jnp.float32)
+        for q in range(reps):
+            at = s * rows + q * part
+            packed = jnp.where(grp == q, res[at : at + part, LANES:], packed)
+        lgs[s] = packed
+    long_sent = ship(3, lambda peer: lgs.at[peer], lgr.at[me])
+    lgr[me] = lgs[me]
+    key_grads = res[:, :LANES] * feature(2)
+    finish(1, key_grads, igs.at[1])
+    key_sent = ship(4, lambda peer: igs.at[1, peer], igr.at[1, me])
+    value_grads = res[:, :LANES] * feature(1)
+    finish(2, value_grads, igs.at[2])
+    value_sent = ship(5, lambda peer: igs.at[2, peer], igr.at[2, me])
+
+    @pl.loop(0, tokens // chunk)
+    def _(i):
+        at = pl.ds(pl.multiple_of(i * chunk, chunk), chunk)
+        total = paired(ch[at, :], cl[at, :], ec) + paired(sh[at, :], sl[at, :], oc)
+        row = lax.broadcasted_iota(jnp.int32, total.shape, 0)
+        res0[at, :] = total + jnp.where(row % 2 == 0, conv_end, -conv_end)
+
+    query_grads = stream(3) * res0[...]
+    finish(0, query_grads, igs.at[0])
+    query_sent = ship(6, lambda peer: igs.at[0, peer], igr.at[0, me])
+    tap_lines(0, query_grads)
+    tap_lines(1, res[:, :LANES] * feature(2))
+    tap_lines(2, res[:, :LANES] * feature(1))
+    taps_sent = ship(7, lambda peer: tgs, tgr.at[me])
+    tgr[me] = tgs[...]
+    for p in range(streams):
+        igr[p, me] = igs[p, me]
+    for copy in long_sent:
+        copy.wait()
+    per = n // m
+    chan_sent = []
+    for j in range(1, m):
+        peer = lax.rem(mine + j, m)
+        copy = pltpu.make_async_remote_copy(
+            src_ref=lgr.at[pl.ds(peer * per, per)], dst_ref=l2.at[mine], send_sem=csems.at[0, j - 1],
+            recv_sem=csems.at[1, j - 1], device_id={"chan": peer}, device_id_type=MESH,
+        )
+        copy.start()
+        chan_sent.append(copy)
+    l2[mine] = lgr[pl.ds(mine * per, per)]
+
+    def put_stream(p):
+        for h in range(tiles):
+            joined = jnp.concatenate([igr[p, h * reps + g] for g in range(reps)], axis=1)
+            moved = dot(joined, swap).astype(jnp.bfloat16)
+            for r in range(reps):
+                at = (r * tiles + h) * LANES
+                out_ref[p, :, at : at + LANES] = moved[:, r * LANES : (r + 1) * LANES]
+
+    for copy in key_sent:
+        copy.wait()
+    put_stream(1)
+    for copy in value_sent:
+        copy.wait()
+    put_stream(2)
+    for copy in chan_sent:
+        copy.wait()
+    total = l2[0]
+    for k in range(1, m):
+        total = total + l2[k]
+    for q in range(reps):
+        line = jnp.zeros((part, LANES), jnp.float32)
+        for k in range(per):
+            line = jnp.where(grp == k, turn(total[k], (k - q) * width, 1), line)
+        lo_ref[q * part : (q + 1) * part, :] = line[:, : per * width]
+    for copy in query_sent:
+        copy.wait()
+    put_stream(0)
+    for copy in taps_sent:
+        copy.wait()
+    for h in range(tiles):
+        for r in range(reps):
+            line = jnp.zeros((16, LANES), jnp.float32)
+            for g in range(reps):
+                moved = turn(tgr[h * reps + g], (g - r) * width, 1)
+                line = jnp.where(lane_group(16, width) == g, moved, line)
+            at = (r * tiles + h) * LANES
+            for p in range(streams):
+                to_ref[p, :, at : at + LANES] = line[tap_count * p : tap_count * (p + 1)]
+
+
+def whole_specs(count):
+    return [pl.BlockSpec(memory_space=pltpu.VMEM)] * count
+
+
+def half_tables(tokens):
+    step = 32
+    col = np.arange(tokens)
+    coarse = np.arange(tokens // step)[:, None] * step * col[None, :] % (2 * tokens)
+    fine = np.arange(step)[:, None] * col[None, :] % (2 * tokens)
+    out = []
+    for index in (coarse, fine):
+        phase = index * (math.pi / tokens)
+        out += [np.cos(phase).astype(np.float32), np.sin(phase).astype(np.float32)]
+    return out
+
+
+def fast_shards(n, m, proj_in, taps, long_filter, out_grad):
+    streams, rows, channels = proj_in.shape
+    groups = long_filter.shape[1]
+    reps = channels // groups
+    part = rows // reps
+    tokens = n * rows
+    f32, bf16 = jnp.float32, jnp.bfloat16
+    shape, vmem = jax.ShapeDtypeStruct, pltpu.VMEM
+    wide = vmem((tokens, 2 * LANES), bf16)
+    full = vmem((tokens, 2 * LANES), f32)
+    packs = vmem((n, part, LANES), f32)
+    moved = vmem((2, n, 2, rows, LANES), bf16)
+    grads = vmem((streams, n, rows, LANES), bf16)
+    return pl.pallas_call(
+        functools.partial(whole_kernel, n, m, reps),
+        out_shape=(
+            shape((streams, rows, channels), bf16), shape((rows, groups // m), f32), shape(taps.shape, f32),
+        ),
+        in_specs=whole_specs(8),
+        out_specs=whole_specs(3),
+        scratch_shapes=[moved, moved, packs, packs]
+        + [vmem((tokens, tokens), bf16)] * 4
+        + [wide] * 3 + [full] * 2 + [wide] * 6 + [full, vmem((tokens, LANES), f32)]
+        + [grads, grads, packs, packs, vmem((m, n // m, part, LANES), f32)]
+        + [vmem((16, LANES), f32), vmem((n, 16, LANES), f32)]
+        + [pltpu.SemaphoreType.DMA((2, 8, n - 1)), pltpu.SemaphoreType.DMA((2, m - 1))],
+        compiler_params=pltpu.CompilerParams(
+            collective_id=0, has_side_effects=True, vmem_limit_bytes=56 << 20
+        ),
+    )(proj_in, out_grad, long_filter, taps, *half_tables(tokens))
+
+
+def fits(n, m, proj_in, taps, long_filter, out_grad):
+    streams, rows, channels = proj_in.shape
+    groups = long_filter.shape[1]
+    if channels % groups or groups % n or n % m or streams != 3 or taps.shape[1] != 3:
+        return False
+    reps, width = channels // groups, groups // n
+    if reps < 2 or reps * width != LANES or n % reps or rows % (8 * reps) or rows % 16:
+        return False
+    return n * rows <= TABLE_LIMIT and n * rows % 256 == 0
+
+
+def routed(n, m, *arrays):
+    return fast_shards(n, m, *arrays) if fits(n, m, *arrays) else shards(*arrays)
+
+
 def solution(mesh):
     return jax.shard_map(
-        shards,
+        functools.partial(routed, mesh.shape["seq"], mesh.shape["chan"]),
         mesh=mesh,
         in_specs=(P(None, "seq", "chan"), P(None, None, "chan"), P("seq", None), P("seq", "chan")),
         out_specs=(P(None, "seq", "chan"), P("seq", "chan"), P(None, None, "chan")),

time: 265 us -> 70.8 us (0.27); the launches traced: 261 us -> 70.6 us
  blocking collectives: 87.9 us -> 0 us
  Pallas kernels: 0 us -> 65.7 us
  matrix products: 50.1 us -> 0 us
  waiting for transfers between devices: 48.2 us -> 0 us
  other arithmetic: 23.7 us -> 0 us
  local copies, waits for them, and re-layouts: 24.4 us -> 4.23 us
  between operations: 14.5 us -> 0.64 us
  starting transfers between devices: 11.6 us -> 0 us
    pallas_call x0 -> x1, Pallas kernels: none -> 65.7 us  [fast_shards(): pl.pallas_call(functools.partial(whole_kernel, n, m, reps), out_shape=(sh...]
    all_to_all x1 -> x0, blocking collectives: 52.2 us -> none  [whole_inverse(): lax.all_to_all(signal, 'seq', split_axis=0, concat_axis=2, tiled=True)]
    dot_general x12 -> x0, matrix products: 50.1 us -> none  [contract(): jnp.einsum(pattern, factor_table, operand, precision=lax.Precision.HIGHEST)]
    all_to_all x1 -> x0, waiting for transfers between devices: 47.4 us -> none  [whole_forward(): lax.all_to_all(signal, 'seq', split_axis=2, concat_axis=0, tiled=True)]
    psum x1 -> x0, blocking collectives: 35.7 us -> none  [shards(): tap_grad = lax.psum(partial_taps, 'seq') / math.sqrt(seq_width * tok_rows)]
    unnamed x27 -> x4, local copies, waits for them, and re-layouts: 9.76 us -> 2.69 us
    reduce_sum x2 -> x0, other arithmetic: 6.91 us -> none  [the longest x1 5.18 us: shards(): jnp.sum(feature_grad * lagged[lag_step], axis=1)]
    ppermute x2 -> x0, starting transfers between devices: 6.16 us -> none  [shifted(): return lax.ppermute(x, axis, pairs)]
  transfers between devices with their start and end apart: 4 -> 0, of which waited for: 2 -> 0; matrix products, arithmetic and copies ran while one was open for 9% -> 0% of each run, Pallas kernels for 0% -> 0%
where the time goes in v2:
time: 70.8 us; the launch traced here: 70.6 us
  Pallas kernels  65.7 us (93%)
  local copies, waits for them, and re-layouts  4.23 us (6%)
    pallas_call x1, Pallas kernels, fast_shards(): pl.pallas_call(functools.partial(whole_kernel, n, m, reps), out_shape=(sh...  65.7 us
    unnamed x4, local copies, waits for them, and re-layouts  2.69 us
    pallas_call x1, local copies, waits for them, and re-layouts, fast_shards(): pl.pallas_call(functools.partial(whole_kernel, n, m, reps), out_shape=(sh...  1.54 us

profile of v2, /device:TPU:0, one launch (start us, length us, event | category | flops | bytes accessed | tf_op | source)
XLA Modules:
  0.0 70.6 jit_solution(663975097942877049)
XLA Ops:
  0.6 65.7 %shard_map.103 = (bf16[3,128,1024]{2,1,0:T(8,128)(2,1)}, f32[128,64]{1,0:T(8,128)}, f32[3,3,1024]{2,1,0:T(4,128)}) custom-call(bf16[3,128,1024]{2,1,0:T(8,128)(2,1)} %x_ref.1, bf16[128,1024]{1,0:T(8,128)(2,1)} %og_ref.1, f32[128,256]{1,0:T(8,128)} %lf_ref.1, f32[3,3,1024]{2,1,0:T(4,128)} %tp_ref.1, f32[32,1024]{1,0:T(8,128)} %constant.8.clone.ca, ...), custom_call_target="tpu_custom_call" | custom-call | tf_op jit(solution)/shard_map/pallas_call | solution.py:500
  66.4 1.5 %copy.11 = f32[128,64]{0,1:T(8,128)} copy(f32[128,64]{1,0:T(8,128)} %get-tuple-element.4) | data formatting | bytes 65536 | tf_op jit(solution)/shard_map/pallas_call | solution.py:500
  67.9 0.0 copy-start
  67.9 2.1 %copy.14 = bf16[3,128,1024]{2,1,0:T(8,128)(2,1)} copy(bf16[3,128,1024]{2,1,0:T(8,128)(2,1)} %get-tuple-element.9) | data formatting | bytes 1572864
  70.0 0.0 copy-done
  70.0 0.6 copy.15
Async XLA Ops:
  67.9 2.1 %copy-start = (f32[3,3,1024]{2,1,0:T(4,128)S(1)}, f32[3,3,1024]{2,1,0:T(4,128)}, u32[]{:S(2)}) copy-start(f32[3,3,1024]{2,1,0:T(4,128)} %get-tuple-element.11) | copy-start | bytes 110596

commit v3 on v2

--- a/solution.py
+++ b/solution.py
@@ -251,8 +251,8 @@
             for g in range(reps):
                 xs[place // 2, h * reps + g, place % 2] = moved[:, g * LANES : (g + 1) * LANES]
 
-    gather_stream(x_ref.at[1], 0)
-    gather_stream(x_ref.at[2], 1)
+    gather_stream(x_ref.at[0], 0)
+    gather_stream(og_ref, 1)
     first = ship(0, lambda peer: xs.at[0, peer], xr.at[0, me])
     for s in range(n):
         base = (s // reps) * LANES
@@ -262,8 +262,8 @@
             packed = jnp.where(grp == q, turn(tile, (q - s % reps) * width, 1), packed)
         fs[s] = packed
     first += ship(1, lambda peer: fs.at[peer], fr.at[me])
-    gather_stream(x_ref.at[0], 2)
-    gather_stream(og_ref, 3)
+    gather_stream(x_ref.at[1], 2)
+    gather_stream(x_ref.at[2], 3)
     second = ship(2, lambda peer: xs.at[1, peer], xr.at[1, me])
     xr[0, me] = xs[0, me]
     xr[1, me] = xs[1, me]
@@ -284,7 +284,7 @@
     tgs[...] = jnp.zeros_like(tgs)
     make_table(ca, sa, cb, sb, ch, cl, sh, sl)
 
-    places = {1: (0, 0), 2: (0, 1), 0: (1, 0), 3: (1, 1)}
+    places = {0: (0, 0), 3: (0, 1), 1: (1, 0), 2: (1, 1)}
 
     def stream(p):
         half, at = places[p]
@@ -315,9 +315,9 @@
     for copy in first:
         copy.wait()
     sign = alternating(tokens)
-    mixed = feature(1) * feature(2)
-    mh[:, :LANES], ml[:, :LANES] = halves(mixed)
-    mixed_end = jnp.sum(sign * mixed, axis=0, keepdims=True)
+    grad = stream(3) * feature(0)
+    mh[:, :LANES], ml[:, :LANES] = halves(grad)
+    grad_end = jnp.sum(sign * grad, axis=0, keepdims=True)
     filt_end = jnp.zeros((1, LANES), jnp.float32)
     for s in range(n):
         packed = fr[s]
@@ -334,33 +334,59 @@
         a = three(ch[at, :], cl[at, :], mh[...], ml[...])
         b = three(sh[at, :], sl[at, :], mh[...], ml[...])
         sa_f[at, :], sb_f[at, :] = a, b
-        am, af, bm, bf = a[:, :LANES], a[:, LANES:], b[:, :LANES], b[:, LANES:]
+        ag, af, bg, bf = a[:, :LANES], a[:, LANES:], b[:, :LANES], b[:, LANES:]
         weight = weight_of(i, chunk)
-        ec[at, :LANES], ec[at, LANES:] = halves((af * am - bf * bm) * weight)
-        oc[at, :LANES], oc[at, LANES:] = halves((af * bm + bf * am) * weight)
-
-    for copy in second:
-        copy.wait()
-    grad = stream(3) * feature(0)
-    gg[:, :LANES], gg[:, LANES:] = halves(grad)
-    grad_end = jnp.sum(sign * grad, axis=0, keepdims=True)
+        ec[at, :LANES], ec[at, LANES:] = halves((af * ag + bf * bg) * weight)
+        oc[at, :LANES], oc[at, LANES:] = halves((af * bg - bf * ag) * weight)
+
+    back_end = filt_end * grad_end * (0.5 / tokens)
 
     @pl.loop(0, tokens // chunk)
     def _(i):
         at = pl.ds(pl.multiple_of(i * chunk, chunk), chunk)
-        ag = paired(ch[at, :], cl[at, :], gg)
-        bg = paired(sh[at, :], sl[at, :], gg)
-        am, af, bm, bf = sa_f[at, :LANES], sa_f[at, LANES:], sb_f[at, :LANES], sb_f[at, LANES:]
+        total = paired(ch[at, :], cl[at, :], ec) + paired(sh[at, :], sl[at, :], oc)
+        row = lax.broadcasted_iota(jnp.int32, total.shape, 0)
+        res0[at, :] = total + jnp.where(row % 2 == 0, back_end, -back_end)
+
+    for copy in second:
+        copy.wait()
+
+    def finish(p, grads, place):
+        total = taps[p][0] * grads
+        for lag in range(1, tap_count):
+            total = total + taps[p][lag] * sooner(grads, lag)
+        place[...] = total.astype(jnp.bfloat16).reshape(n, rows, LANES)
+
+    def tap_lines(p, grads):
+        x = stream(p)
+        for lag in range(tap_count):
+            line = jnp.sum(grads * later(x, lag), axis=0, keepdims=True)
+            tgs[tap_count * p + lag : tap_count * p + lag + 1, :] = line * (1.0 / math.sqrt(tokens))
+
+    key_rows, value_rows = feature(1), feature(2)
+    mixed = key_rows * value_rows
+    gg[:, :LANES], gg[:, LANES:] = halves(mixed)
+    mixed_end = jnp.sum(sign * mixed, axis=0, keepdims=True)
+    finish(1, res0[...] * value_rows, igs.at[1])
+    key_sent = ship(4, lambda peer: igs.at[1, peer], igr.at[1, me])
+    finish(2, res0[...] * key_rows, igs.at[2])
+    value_sent = ship(5, lambda peer: igs.at[2, peer], igr.at[2, me])
+
+    @pl.loop(0, tokens // chunk)
+    def _(i):
+        at = pl.ds(pl.multiple_of(i * chunk, chunk), chunk)
+        am = paired(ch[at, :], cl[at, :], gg)
+        bm = paired(sh[at, :], sl[at, :], gg)
+        ag, af, bg, bf = sa_f[at, :LANES], sa_f[at, LANES:], sb_f[at, :LANES], sb_f[at, LANES:]
         weight = weight_of(i, chunk)
-        eh[at, :LANES], el[at, :LANES] = halves((af * ag + bf * bg) * weight)
-        oh[at, :LANES], ol[at, :LANES] = halves((af * bg - bf * ag) * weight)
+        eh[at, :LANES], el[at, :LANES] = halves((af * am - bf * bm) * weight)
+        oh[at, :LANES], ol[at, :LANES] = halves((af * bm + bf * am) * weight)
         eh[at, LANES:], el[at, LANES:] = halves(group_sum(ag * am + bg * bm, reps) * weight)
         oh[at, LANES:], ol[at, LANES:] = halves(group_sum(bg * am - ag * bm, reps) * weight)
 
     ends = jnp.concatenate(
-        [filt_end * grad_end, group_sum(grad_end * mixed_end, reps)], axis=1
+        [filt_end * mixed_end, group_sum(grad_end * mixed_end, reps)], axis=1
     ) * (0.5 / tokens)
-    conv_end = filt_end * mixed_end * (0.5 / tokens)
 
     @pl.loop(0, tokens // chunk)
     def _(i):
@@ -369,18 +395,6 @@
         total = total + three(sh[at, :], sl[at, :], oh[...], ol[...])
         row = lax.broadcasted_iota(jnp.int32, total.shape, 0)
         res[at, :] = total + jnp.where(row % 2 == 0, ends, -ends)
-
-    def finish(p, grads, place):
-        total = taps[p][0] * grads
-        for lag in range(1, tap_count):
-            total = total + taps[p][lag] * sooner(grads, lag)
-        place[...] = total.astype(jnp.bfloat16).reshape(n, rows, LANES)
-
-    def tap_lines(p, grads):
-        x = stream(p)
-        for lag in range(tap_count):
-            line = jnp.sum(grads * later(x, lag), axis=0, keepdims=True)
-            tgs[tap_count * p + lag : tap_count * p + lag + 1, :] = line * (1.0 / math.sqrt(tokens))
 
     for s in range(n):
         packed = jnp.zeros((part, LANES), jnp.float32)
@@ -390,26 +404,12 @@
         lgs[s] = packed
     long_sent = ship(3, lambda peer: lgs.at[peer], lgr.at[me])
     lgr[me] = lgs[me]
-    key_grads = res[:, :LANES] * feature(2)
-    finish(1, key_grads, igs.at[1])
-    key_sent = ship(4, lambda peer: igs.at[1, peer], igr.at[1, me])
-    value_grads = res[:, :LANES] * feature(1)
-    finish(2, value_grads, igs.at[2])
-    value_sent = ship(5, lambda peer: igs.at[2, peer], igr.at[2, me])
-
-    @pl.loop(0, tokens // chunk)
-    def _(i):
-        at = pl.ds(pl.multiple_of(i * chunk, chunk), chunk)
-        total = paired(ch[at, :], cl[at, :], ec) + paired(sh[at, :], sl[at, :], oc)
-        row = lax.broadcasted_iota(jnp.int32, total.shape, 0)
-        res0[at, :] = total + jnp.where(row % 2 == 0, conv_end, -conv_end)
-
-    query_grads = stream(3) * res0[...]
+    query_grads = stream(3) * res[:, :LANES]
     finish(0, query_grads, igs.at[0])
     query_sent = ship(6, lambda peer: igs.at[0, peer], igr.at[0, me])
     tap_lines(0, query_grads)
-    tap_lines(1, res[:, :LANES] * feature(2))
-    tap_lines(2, res[:, :LANES] * feature(1))
+    tap_lines(1, res0[...] * feature(2))
+    tap_lines(2, res0[...] * feature(1))
     taps_sent = ship(7, lambda peer: tgs, tgr.at[me])
     tgr[me] = tgs[...]
     for p in range(streams):

time: 70.8 us -> 66.2 us (0.935)
  Pallas kernels: 65.7 us -> 61.1 us
    pallas_call x1, Pallas kernels: 65.7 us -> 61.1 us  [fast_shards(): pl.pallas_call(functools.partial(whole_kernel, n, m, reps), out_shape=(sh...]
where the time goes in v3:
time: 66.2 us; the launch traced here: 66 us
  Pallas kernels  61.1 us (92%)
  local copies, waits for them, and re-layouts  4.23 us (6%)
    pallas_call x1, Pallas kernels, fast_shards(): pl.pallas_call(functools.partial(whole_kernel, n, m, reps), out_shape=(sh...  61.1 us
    unnamed x4, local copies, waits for them, and re-layouts  2.69 us
    pallas_call x1, local copies, waits for them, and re-layouts, fast_shards(): pl.pallas_call(functools.partial(whole_kernel, n, m, reps), out_shape=(sh...  1.54 us

profile of v3, /device:TPU:0, one launch (start us, length us, event | category | flops | bytes accessed | tf_op | source)
XLA Modules:
  0.0 66.0 jit_solution(18037124664437953773)
XLA Ops:
  0.6 61.1 %shard_map.103 = (bf16[3,128,1024]{2,1,0:T(8,128)(2,1)}, f32[128,64]{1,0:T(8,128)}, f32[3,3,1024]{2,1,0:T(4,128)}) custom-call(bf16[3,128,1024]{2,1,0:T(8,128)(2,1)} %x_ref.1, bf16[128,1024]{1,0:T(8,128)(2,1)} %og_ref.1, f32[128,256]{1,0:T(8,128)} %lf_ref.1, f32[3,3,1024]{2,1,0:T(4,128)} %tp_ref.1, f32[32,1024]{1,0:T(8,128)} %constant.8.clone.ca, ...), custom_call_target="tpu_custom_call" | custom-call | tf_op jit(solution)/shard_map/pallas_call | solution.py:500
  61.8 1.5 %copy.11 = f32[128,64]{0,1:T(8,128)} copy(f32[128,64]{1,0:T(8,128)} %get-tuple-element.4) | data formatting | bytes 65536 | tf_op jit(solution)/shard_map/pallas_call | solution.py:500
  63.3 0.0 copy-start
  63.3 2.1 %copy.14 = bf16[3,128,1024]{2,1,0:T(8,128)(2,1)} copy(bf16[3,128,1024]{2,1,0:T(8,128)(2,1)} %get-tuple-element.9) | data formatting | bytes 1572864
  65.4 0.0 copy-done
  65.4 0.6 copy.15
Async XLA Ops:
  63.3 2.1 %copy-start = (f32[3,3,1024]{2,1,0:T(4,128)S(1)}, f32[3,3,1024]{2,1,0:T(4,128)}, u32[]{:S(2)}) copy-start(f32[3,3,1024]{2,1,0:T(4,128)} %get-tuple-element.11) | copy-start | bytes 110596

commit v4 on v3

--- a/solution.py
+++ b/solution.py
@@ -215,7 +215,7 @@
 def whole_kernel(
     n, m, reps, x_ref, og_ref, lf_ref, tp_ref, ca, sa, cb, sb, out_ref, lo_ref, to_ref,
     xs, xr, fs, fr, ch, cl, sh, sl, mh, ml, gg, sa_f, sb_f, eh, el, oh, ol, ec, oc, res, res0,
-    igs, igr, lgs, lgr, l2, tgs, tgr, sems, csems,
+    igs, igr, lgs, lgc, lsum, lgr, l2, tgs, tgr, sems, csems,
 ):
     me, mine = lax.axis_index("seq"), lax.axis_index("chan")
     width = LANES // reps
@@ -223,6 +223,7 @@
     tap_count = tp_ref.shape[1]
     tokens = n * rows
     part = rows // reps
+    share = part // m
     tiles = n // reps
     meet([("seq", n), ("chan", m)])
     grp = lane_group(part, width)
@@ -239,6 +240,18 @@
             copies.append(copy)
         return copies
 
+    def spread(kind, source, target):
+        copies = []
+        for j in range(1, m):
+            peer = lax.rem(mine + j, m)
+            copy = pltpu.make_async_remote_copy(
+                src_ref=source(peer), dst_ref=target, send_sem=csems.at[0, kind, j - 1],
+                recv_sem=csems.at[1, kind, j - 1], device_id={"chan": peer}, device_id_type=MESH,
+            )
+            copy.start()
+            copies.append(copy)
+        return copies
+
     swap = swap_matrix(reps, width)
 
     def gather_stream(source, place):
@@ -251,23 +264,23 @@
             for g in range(reps):
                 xs[place // 2, h * reps + g, place % 2] = moved[:, g * LANES : (g + 1) * LANES]
 
-    gather_stream(x_ref.at[0], 0)
-    gather_stream(og_ref, 1)
-    first = ship(0, lambda peer: xs.at[0, peer], xr.at[0, me])
     for s in range(n):
         base = (s // reps) * LANES
         packed = jnp.zeros((part, LANES), jnp.float32)
         for q in range(reps):
             tile = lf_ref[q * part : (q + 1) * part, base : base + LANES]
             packed = jnp.where(grp == q, turn(tile, (q - s % reps) * width, 1), packed)
-        fs[s] = packed
-    first += ship(1, lambda peer: fs.at[peer], fr.at[me])
+        fs[s] = packed.reshape(m, share, LANES)
+    filter_sent = ship(1, lambda peer: fs.at[peer, mine], fr.at[mine, me])
+    gather_stream(x_ref.at[0], 0)
+    gather_stream(og_ref, 1)
+    first = ship(0, lambda peer: xs.at[0, peer], xr.at[0, me])
     gather_stream(x_ref.at[1], 2)
     gather_stream(x_ref.at[2], 3)
     second = ship(2, lambda peer: xs.at[1, peer], xr.at[1, me])
     xr[0, me] = xs[0, me]
     xr[1, me] = xs[1, me]
-    fr[me] = fs[me]
+    fr[mine, me] = fs[me, mine]
 
     taps = []
     home, slot = me // reps, lax.rem(me, reps)
@@ -284,6 +297,10 @@
     tgs[...] = jnp.zeros_like(tgs)
     make_table(ca, sa, cb, sb, ch, cl, sh, sl)
 
+    for copy in filter_sent:
+        copy.wait()
+    filter_passed = spread(0, lambda peer: fr.at[mine], fr.at[mine])
+
     places = {0: (0, 0), 3: (0, 1), 1: (1, 0), 2: (1, 1)}
 
     def stream(p):
@@ -319,8 +336,10 @@
     mh[:, :LANES], ml[:, :LANES] = halves(grad)
     grad_end = jnp.sum(sign * grad, axis=0, keepdims=True)
     filt_end = jnp.zeros((1, LANES), jnp.float32)
+    for copy in filter_passed:
+        copy.wait()
     for s in range(n):
-        packed = fr[s]
+        packed = jnp.concatenate([fr[k, s] for k in range(m)], axis=0)
         for q in range(reps):
             piece = group_sum(jnp.where(grp == q, packed, 0.0), reps)
             filt_end = filt_end + jnp.sum(alternating(part) * piece, axis=0, keepdims=True)
@@ -401,11 +420,20 @@
         for q in range(reps):
             at = s * rows + q * part
             packed = jnp.where(grp == q, res[at : at + part, LANES:], packed)
-        lgs[s] = packed
-    long_sent = ship(3, lambda peer: lgs.at[peer], lgr.at[me])
-    lgr[me] = lgs[me]
+        for k in range(m):
+            lgs[k, s] = packed[k * share : (k + 1) * share]
+    long_parts = spread(1, lambda peer: lgs.at[peer], lgc.at[mine])
+    lgc[mine] = lgs[mine]
     query_grads = stream(3) * res[:, :LANES]
     finish(0, query_grads, igs.at[0])
+    for copy in long_parts:
+        copy.wait()
+    summed = lgc[0]
+    for k in range(1, m):
+        summed = summed + lgc[k]
+    lsum[...] = summed
+    long_sent = ship(3, lambda peer: lsum.at[peer], lgr.at[me])
+    lgr[me] = lsum[me]
     query_sent = ship(6, lambda peer: igs.at[0, peer], igr.at[0, me])
     tap_lines(0, query_grads)
     tap_lines(1, res0[...] * feature(2))
@@ -417,15 +445,7 @@
     for copy in long_sent:
         copy.wait()
     per = n // m
-    chan_sent = []
-    for j in range(1, m):
-        peer = lax.rem(mine + j, m)
-        copy = pltpu.make_async_remote_copy(
-            src_ref=lgr.at[pl.ds(peer * per, per)], dst_ref=l2.at[mine], send_sem=csems.at[0, j - 1],
-            recv_sem=csems.at[1, j - 1], device_id={"chan": peer}, device_id_type=MESH,
-        )
-        copy.start()
-        chan_sent.append(copy)
+    chan_sent = spread(2, lambda peer: lgr.at[pl.ds(peer * per, per)], l2.at[mine])
     l2[mine] = lgr[pl.ds(mine * per, per)]
 
     def put_stream(p):
@@ -444,14 +464,14 @@
     put_stream(2)
     for copy in chan_sent:
         copy.wait()
-    total = l2[0]
-    for k in range(1, m):
-        total = total + l2[k]
+    sources = [jnp.concatenate([l2[q, k] for q in range(m)], axis=0) for k in range(per)]
+    lines = []
     for q in range(reps):
         line = jnp.zeros((part, LANES), jnp.float32)
         for k in range(per):
-            line = jnp.where(grp == k, turn(total[k], (k - q) * width, 1), line)
-        lo_ref[q * part : (q + 1) * part, :] = line[:, : per * width]
+            line = jnp.where(grp == k, turn(sources[k], (k - q) * width, 1), line)
+        lines.append(line)
+    lo_ref[...] = jnp.concatenate(lines, axis=0).T[: per * width]
     for copy in query_sent:
         copy.wait()
     put_stream(0)
@@ -494,26 +514,29 @@
     shape, vmem = jax.ShapeDtypeStruct, pltpu.VMEM
     wide = vmem((tokens, 2 * LANES), bf16)
     full = vmem((tokens, 2 * LANES), f32)
-    packs = vmem((n, part, LANES), f32)
+    share = part // m
+    quarters = vmem((m, n, share, LANES), f32)
+    quarter = vmem((n, share, LANES), f32)
     moved = vmem((2, n, 2, rows, LANES), bf16)
     grads = vmem((streams, n, rows, LANES), bf16)
-    return pl.pallas_call(
+    out, long_grad, tap_grad = pl.pallas_call(
         functools.partial(whole_kernel, n, m, reps),
         out_shape=(
-            shape((streams, rows, channels), bf16), shape((rows, groups // m), f32), shape(taps.shape, f32),
+            shape((streams, rows, channels), bf16), shape((groups // m, rows), f32), shape(taps.shape, f32),
         ),
         in_specs=whole_specs(8),
         out_specs=whole_specs(3),
-        scratch_shapes=[moved, moved, packs, packs]
+        scratch_shapes=[moved, moved, vmem((n, m, share, LANES), f32), quarters]
         + [vmem((tokens, tokens), bf16)] * 4
         + [wide] * 3 + [full] * 2 + [wide] * 6 + [full, vmem((tokens, LANES), f32)]
-        + [grads, grads, packs, packs, vmem((m, n // m, part, LANES), f32)]
+        + [grads, grads, quarters, quarters, quarter, quarter, vmem((m, n // m, share, LANES), f32)]
         + [vmem((16, LANES), f32), vmem((n, 16, LANES), f32)]
-        + [pltpu.SemaphoreType.DMA((2, 8, n - 1)), pltpu.SemaphoreType.DMA((2, m - 1))],
+        + [pltpu.SemaphoreType.DMA((2, 8, n - 1)), pltpu.SemaphoreType.DMA((2, 3, m - 1))],
         compiler_params=pltpu.CompilerParams(
             collective_id=0, has_side_effects=True, vmem_limit_bytes=56 << 20
         ),
     )(proj_in, out_grad, long_filter, taps, *half_tables(tokens))
+    return (out, long_grad.T, tap_grad)
 
 
 def fits(n, m, proj_in, taps, long_filter, out_grad):
@@ -522,7 +545,7 @@
     if channels % groups or groups % n or n % m or streams != 3 or taps.shape[1] != 3:
         return False
     reps, width = channels // groups, groups // n
-    if reps < 2 or reps * width != LANES or n % reps or rows % (8 * reps) or rows % 16:
+    if reps < 2 or reps * width != LANES or n % reps or rows % (8 * reps * m) or rows % LANES:
         return False
     return n * rows <= TABLE_LIMIT and n * rows % 256 == 0
 

time: 66.2 us -> 63.2 us (0.955)
  Pallas kernels: 61.1 us -> 58.8 us
  local copies, waits for them, and re-layouts: 4.23 us -> 3.5 us
    pallas_call x1, Pallas kernels: 61.1 us -> 58.8 us  [fast_shards(): pl.pallas_call(functools.partial(whole_kernel, n, m, reps), out_shape=(sh...]
    pallas_call x1 -> x0, local copies, waits for them, and re-layouts: 1.54 us -> none  [fast_shards(): pl.pallas_call(functools.partial(whole_kernel, n, m, reps), out_shape=(sh...]
    unnamed x4 -> x7, local copies, waits for them, and re-layouts: 2.69 us -> 3.5 us
where the time goes in v4:
time: 63.2 us; the launch traced here: 63 us
  Pallas kernels  58.8 us (93%)
  local copies, waits for them, and re-layouts  3.5 us (6%)
  between operations  0.65 us (1%)
    pallas_call x1, Pallas kernels, fast_shards(): pl.pallas_call(functools.partial(whole_kernel, n, m, reps), out_shape=(sh...  58.8 us
    unnamed x7, local copies, waits for them, and re-layouts  3.5 us

profile of v4, /device:TPU:0, one launch (start us, length us, event | category | flops | bytes accessed | tf_op | source)
XLA Modules:
  0.0 63.0 jit_solution(5814995504125601324)
XLA Ops:
  0.6 58.8 %shard_map.103 = (bf16[3,128,1024]{2,1,0:T(8,128)(2,1)}, f32[64,128]{1,0:T(8,128)}, f32[3,3,1024]{2,1,0:T(4,128)}) custom-call(bf16[3,128,1024]{2,1,0:T(8,128)(2,1)} %x_ref.1, bf16[128,1024]{1,0:T(8,128)(2,1)} %og_ref.1, f32[128,256]{1,0:T(8,128)} %lf_ref.1, f32[3,3,1024]{2,1,0:T(4,128)} %tp_ref.1, f32[32,1024]{1,0:T(8,128)} %constant.8.clone.ca, ...), custom_call_target="tpu_custom_call" | custom-call | tf_op jit(solution)/shard_map/pallas_call | solution.py:522
  59.5 0.0 copy-start.1
  59.5 2.1 %copy.14 = bf16[3,128,1024]{2,1,0:T(8,128)(2,1)} copy(bf16[3,128,1024]{2,1,0:T(8,128)(2,1)} %get-tuple-element.12) | data formatting | bytes 1572864
  61.6 0.0 copy-done.1
  61.6 0.0 copy-start
  61.6 0.6 copy.15
  62.2 0.2 copy-done
  62.4 0.6 copy.16
Async XLA Ops:
  59.5 2.1 %copy-start.1 = (f32[64,128]{1,0:T(8,128)S(1)}, f32[64,128]{1,0:T(8,128)}, u32[]{:S(2)}) copy-start(f32[64,128]{1,0:T(8,128)} %get-tuple-element.7) | copy-start | bytes 98308
  61.6 0.8 %copy-start = (f32[3,3,1024]{2,1,0:T(4,128)S(1)}, f32[3,3,1024]{2,1,0:T(4,128)}, u32[]{:S(2)}) copy-start(f32[3,3,1024]{2,1,0:T(4,128)} %get-tuple-element.14) | copy-start | bytes 110596

commit v5 on v4

--- a/solution.py
+++ b/solution.py
@@ -230,7 +230,7 @@
 
     def ship(kind, source, target):
         copies = []
-        for j in range(1, n):
+        for j in sorted(range(1, n), key=lambda j: abs(2 * j - n)):
             peer = lax.rem(me + j, n)
             copy = pltpu.make_async_remote_copy(
                 src_ref=source(peer), dst_ref=target, send_sem=sems.at[0, kind, j - 1],

time: 63.2 us -> 61.6 us (0.975)
  Pallas kernels: 58.8 us -> 57.3 us
    pallas_call x1, Pallas kernels: 58.8 us -> 57.3 us  [fast_shards(): pl.pallas_call(functools.partial(whole_kernel, n, m, reps), out_shape=(sh...]
where the time goes in v5:
time: 61.6 us; the launch traced here: 61.4 us
  Pallas kernels  57.3 us (93%)
  local copies, waits for them, and re-layouts  3.5 us (6%)
  between operations  0.65 us (1%)
    pallas_call x1, Pallas kernels, fast_shards(): pl.pallas_call(functools.partial(whole_kernel, n, m, reps), out_shape=(sh...  57.3 us
    unnamed x7, local copies, waits for them, and re-layouts  3.5 us

profile of v5, /device:TPU:0, one launch (start us, length us, event | category | flops | bytes accessed | tf_op | source)
XLA Modules:
  0.0 61.4 jit_solution(9000557370349555405)
XLA Ops:
  0.6 57.3 %shard_map.103 = (bf16[3,128,1024]{2,1,0:T(8,128)(2,1)}, f32[64,128]{1,0:T(8,128)}, f32[3,3,1024]{2,1,0:T(4,128)}) custom-call(bf16[3,128,1024]{2,1,0:T(8,128)(2,1)} %x_ref.1, bf16[128,1024]{1,0:T(8,128)(2,1)} %og_ref.1, f32[128,256]{1,0:T(8,128)} %lf_ref.1, f32[3,3,1024]{2,1,0:T(4,128)} %tp_ref.1, f32[32,1024]{1,0:T(8,128)} %constant.8.clone.ca, ...), custom_call_target="tpu_custom_call" | custom-call | tf_op jit(solution)/shard_map/pallas_call | solution.py:522
  57.9 0.0 copy-start.1
  57.9 2.1 %copy.14 = bf16[3,128,1024]{2,1,0:T(8,128)(2,1)} copy(bf16[3,128,1024]{2,1,0:T(8,128)(2,1)} %get-tuple-element.12) | data formatting | bytes 1572864
  60.0 0.0 copy-done.1
  60.0 0.0 copy-start
  60.0 0.6 %copy.15 = f32[128,64]{0,1:T(8,128)} copy(f32[128,64]{0,1:T(8,128)S(1)} %bitcast.1) | data formatting | bytes 65536
  60.6 0.2 copy-done
  60.8 0.6 %copy.16 = f32[3,3,1024]{2,1,0:T(4,128)} copy(f32[3,3,1024]{2,1,0:T(4,128)S(1)} %copy-done) | data formatting | bytes 73728
Async XLA Ops:
  57.9 2.1 %copy-start.1 = (f32[64,128]{1,0:T(8,128)S(1)}, f32[64,128]{1,0:T(8,128)}, u32[]{:S(2)}) copy-start(f32[64,128]{1,0:T(8,128)} %get-tuple-element.7) | copy-start | bytes 98308
  60.0 0.8 %copy-start = (f32[3,3,1024]{2,1,0:T(4,128)S(1)}, f32[3,3,1024]{2,1,0:T(4,128)}, u32[]{:S(2)}) copy-start(f32[3,3,1024]{2,1,0:T(4,128)} %get-tuple-element.14) | copy-start | bytes 110596
